TPU v7x, 256 devices: a whole 4x4x8 slice. The times are simulated.
256 devices in a mesh: grp: 2 (over y_hi), ta: 8 (over y_lo, x), xyz: 16 (over z, core).
Axes of the slice: x: 4, y: 4 (y_hi: 2, y_lo: 2; y = y_hi * 2 + y_lo), z: 8, core: 2. Of those that a mesh axis runs over, the one named last changes fastest.
Arguments:
- right_sides: float32 [4, 24, 8, 32, 256], P('grp', None, 'ta', 'xyz'), may hold values from -6 to 6
- gauge_links: float32 [4, 18, 8, 32, 256], P(None, None, 'ta', 'xyz'), may hold values from -1.8 to 1.8
- eigenvectors: bfloat16 [8, 256, 6, 32, 256], P('ta', 'grp', None, 'xyz'), may hold values from -6 to 6
- step_lengths: float32 [4], replicated, may hold values from 0.6 to 1
Outputs:
- solution: float32 [4, 24, 8, 32, 256], P('grp', None, 'ta', 'xyz')
- correlations: float32 [8, 256, 3, 2, 256], P('ta', 'xyz', None, None, 'grp')
- perambulator: float32 [8, 256, 4, 8], P('ta', 'xyz', 'grp')
All inputs are finite; a program needn't handle non-finite values.
Results may differ from a plain program's by a relative error of at most 0.0029.
Values may be sent and summed in bfloat16 or wider, within the bound.
A program may use at most 128 MiB of HBM per device.

v0:
```python
import functools
import math

import jax
import jax.numpy as jnp
from jax import lax
from jax.experimental import pallas as pl
from jax.experimental.pallas import tpu as pltpu
from jax.sharding import PartitionSpec as P

MESH = pl.DeviceIdType.MESH
F32 = jnp.float32
BF16 = jnp.bfloat16
SX = 16
ITERS = 4
HOPPING = 0.1
GAMMA_TABLE = (
    ((3, 0, 1), (2, 0, 1), (1, 0, -1), (0, 0, -1)),
    ((3, -1, 0), (2, 1, 0), (1, 1, 0), (0, -1, 0)),
    ((2, 0, 1), (3, 0, -1), (0, 0, -1), (1, 0, 1)),
    ((2, 1, 0), (3, 1, 0), (0, 1, 0), (1, 1, 0)),
)


def dot_nt(a, b):
    return lax.dot_general(a, b, (((1,), (1,)), ((), ())), preferred_element_type=F32)


def plus(a, b, sign):
    return a + b if sign > 0 else a - b


def phased(re, im, pr, pi):
    if pi == 0:
        return (pr, re), (pr, im)
    return (-pi, im), (pi, re)


def project(psi, direction, sign):
    re, im = [], []
    for target in range(2):
        source, pr, pi = GAMMA_TABLE[direction][target]
        (s0, a0), (s1, a1) = phased(psi[source][0], psi[source][1], pr, pi)
        re.append(plus(psi[target][0], a0, sign * s0))
        im.append(plus(psi[target][1], a1, sign * s1))
    return jnp.stack(re), jnp.stack(im)


def rebuild(acc, re, im, direction, sign):
    for target in range(4):
        if target < 2:
            terms = ((1, re[target]), (1, im[target]))
        else:
            source, pr, pi = GAMMA_TABLE[direction][target]
            (s0, a0), (s1, a1) = phased(re[source], im[source], pr, pi)
            terms = ((sign * s0, a0), (sign * s1, a1))
        for part in range(2):
            s, a = terms[part]
            old = acc[target][part]
            if old is None:
                acc[target][part] = a if s > 0 else -a
            else:
                acc[target][part] = plus(old, a, s)


def colour(u, re, im, dagger):
    out_re = out_im = None
    for b in range(3):
        ur = u[0, b] if dagger else u[0, :, b]
        ui = u[1, b] if dagger else u[1, :, b]
        vr, vi = re[:, b][:, None], im[:, b][:, None]
        ur, ui = ur[None], ui[None]
        t0 = plus(ur * vr, ui * vi, 1 if dagger else -1)
        t1 = plus(ur * vi, ui * vr, -1 if dagger else 1)
        out_re = t0 if out_re is None else out_re + t0
        out_im = t1 if out_im is None else out_im + t1
    return out_re, out_im


def roll(v, shift, axis):
    shape = v.shape
    flat = v.reshape((-1,) + shape[-2:])
    return pltpu.roll(flat, shift % shape[axis - 2 + len(shape)], axis=1 + axis).reshape(shape)


def kernel(
    sizes, al_ref, rs_ref, u8_ref, lz_ref, v_ref,
    sol_ref, cor_ref, per_ref,
    res, total, hsum, tsend, trecv, zsend, zrecv, w_ref, ub_ref, perm, g_ref, vo_ref, relay, s_ref,
    csend, crecv, psend, precv,
    t_ss, t_rs, z_ss, z_rs, vh_ss, vh_rs, uh_ss, uh_rs, loc_s,
    o_ss, o_rs, r_ss, r_rs, c_ss, c_rs, p_ss, p_rs,
):
    n_grp, n_ta, n_xyz, scale = sizes
    grp = lax.axis_index("grp")
    ta = lax.axis_index("ta")
    me = lax.axis_index("xyz")
    half_ta = n_ta // 2
    y = grp * 2 + ta // half_ta
    x = ta % half_ta

    def y_device(step):
        other = (y + step + 4) % 4
        return (other // 2, (other % 2) * half_ta + x, me)

    y_up, y_down = y_device(1), y_device(-1)
    z_next = (grp, ta, (me + 1) % n_xyz)
    z_prev = (grp, ta, (me + n_xyz - 1) % n_xyz)
    t_next = (grp, (ta + 1) % n_ta, me)
    t_prev = (grp, (ta + n_ta - 1) % n_ta, me)

    barrier = pltpu.get_barrier_semaphore()
    for device in (y_up, y_down, t_next, t_prev):
        pl.semaphore_signal(barrier, inc=1, device_id=device, device_id_type=MESH)

    @pl.loop(1, n_xyz)
    def _(o):
        pl.semaphore_signal(
            barrier, inc=1, device_id=(grp, ta, (me + o) % n_xyz), device_id_type=MESH
        )

    def remote(src, dst, ss, rs, device):
        return pltpu.make_async_remote_copy(
            src_ref=src, dst_ref=dst, send_sem=ss, recv_sem=rs, device_id=device,
            device_id_type=MESH,
        )

    lane = lax.broadcasted_iota(jnp.int32, (8, 128), 1)
    sub = lax.broadcasted_iota(jnp.int32, (8, 128), 0)
    column = lane % SX
    z_is0 = sub % 2 == 0

    def shift_x(v, step):
        if step > 0:
            return jnp.where(column == SX - 1, roll(v, SX - 1, 1), roll(v, -1, 1))
        return jnp.where(column == 0, roll(v, 1 - SX, 1), roll(v, 1, 1))

    def shift_y(v, step):
        a = roll(v, -step * SX, 1)
        keep = lane < 128 - SX if step > 0 else lane >= SX
        return jnp.where(keep, a, roll(a, 4, 0))

    def spins(ref):
        v = ref[...]
        return [[v[6 * s + 3 * p : 6 * s + 3 * p + 3] for p in range(2)] for s in range(4)]

    t_copies = lambda n: (
        remote(tsend.at[n, 0], trecv.at[n, 0], t_ss.at[n, 0], t_rs.at[n, 0], t_prev),
        remote(tsend.at[n, 1], trecv.at[n, 1], t_ss.at[n, 1], t_rs.at[n, 1], t_next),
        remote(zsend.at[n, 0], zrecv.at[n, 0], z_ss.at[n, 0], z_rs.at[n, 0], z_prev),
        remote(zsend.at[n, 1], zrecv.at[n, 1], z_ss.at[n, 1], z_rs.at[n, 1], z_next),
    )

    def prepare(n):
        psi = spins(res)
        re, im = project(psi, 3, -1)
        tsend[n, 0, 0], tsend[n, 0, 1] = re, im
        re, im = colour(u8_ref[3], *project(psi, 3, 1), True)
        tsend[n, 1, 0], tsend[n, 1, 1] = re, im
        re, im = project(psi, 2, -1)
        zsend[n, 0, 0] = jnp.where(z_is0, re[0], roll(re[1], 1, 0))
        zsend[n, 0, 1] = jnp.where(z_is0, im[0], roll(im[1], 1, 0))
        re, im = colour(u8_ref[2], *project(psi, 2, 1), True)
        zsend[n, 1, 0] = jnp.where(z_is0, roll(re[1], 7, 0), re[0])
        zsend[n, 1, 1] = jnp.where(z_is0, roll(im[1], 7, 0), im[0])

    def local_hops():
        psi = spins(res)
        acc = [[None, None] for _ in range(4)]
        for d, shift in ((0, shift_x), (1, shift_y)):
            re, im = project(psi, d, -1)
            rebuild(acc, *colour(u8_ref[d], shift(re, 1), shift(im, 1), False), d, -1)
            re, im = colour(u8_ref[d], *project(psi, d, 1), True)
            rebuild(acc, shift(re, -1), shift(im, -1), d, 1)
        for s in range(4):
            for p in range(2):
                k = 6 * s + 3 * p
                hsum[k : k + 3] = acc[s][p]

    def finish(n):
        psi = spins(res)
        acc = spins(hsum)
        sign_up = jnp.where(ta == n_ta - 1, -1.0, 1.0).astype(F32)
        sign_down = jnp.where(ta == 0, -1.0, 1.0).astype(F32)
        re, im = project(psi, 2, -1)

        def ahead(v, got):
            return jnp.where(z_is0, roll(v, 7, 0), jnp.stack([roll(got, 1, 0), got]))

        re, im = ahead(re, zrecv[n, 0, 0]), ahead(im, zrecv[n, 0, 1])
        rebuild(acc, *colour(u8_ref[2], re, im, False), 2, -1)
        re, im = colour(u8_ref[2], *project(psi, 2, 1), True)

        def behind(v, got):
            return jnp.where(z_is0, jnp.stack([roll(got, 7, 0), got]), roll(v, 1, 0))

        re, im = behind(re, zrecv[n, 1, 0]), behind(im, zrecv[n, 1, 1])
        rebuild(acc, re, im, 2, 1)
        re, im = trecv[n, 0, 0] * sign_up, trecv[n, 0, 1] * sign_up
        rebuild(acc, *colour(u8_ref[3], re, im, False), 3, -1)
        rebuild(acc, trecv[n, 1, 0] * sign_down, trecv[n, 1, 1] * sign_down, 3, 1)
        step = al_ref[n]
        step_after = al_ref[n + 1]
        for s in range(4):
            for p in range(2):
                k = 6 * s + 3 * p
                old = psi[s][p]
                new = old - step * (old - HOPPING * acc[s][p])
                res[k : k + 3] = new
                total[k : k + 3] = total[k : k + 3] + step_after * new

    res[...] = rs_ref[...]
    total[...] = al_ref[0] * rs_ref[...]
    prepare(0)

    pl.semaphore_wait(barrier, n_xyz - 1 + 4)
    for copy in t_copies(0):
        copy.start()
    halo_copies = (
        remote(v_ref.at[:, pl.ds(0, 1536)], w_ref.at[1, 4], vh_ss.at[0], vh_rs.at[0], z_prev),
        remote(v_ref.at[:, pl.ds(1536, 1536)], w_ref.at[0, 5], vh_ss.at[1], vh_rs.at[1], z_next),
        remote(lz_ref.at[1, 2], ub_ref.at[0, 2], uh_ss, uh_rs, z_next),
    )
    for copy in halo_copies:
        copy.start()

    def own_copy(c, direction):
        piece = pl.ds(c * 512, 512)
        return remote(
            v_ref.at[:, piece], relay.at[c], o_ss.at[c], o_rs.at[c],
            y_up if direction == 0 else y_down,
        )

    def relay_copy(c, direction):
        piece = pl.ds(c * 512, 512)
        return remote(
            relay.at[c], vo_ref.at[:, piece], r_ss.at[c], r_rs.at[c],
            y_up if direction == 0 else y_down,
        )

    for c in range(3):
        own_copy(c, 0).start()
        own_copy(c + 3, 1).start()
    local_copies = (
        pltpu.make_async_copy(v_ref.at[:, pl.ds(1536, 1536)], w_ref.at[0, 4], loc_s.at[0]),
        pltpu.make_async_copy(v_ref.at[:, pl.ds(0, 1536)], w_ref.at[1, 5], loc_s.at[1]),
        pltpu.make_async_copy(lz_ref.at[0, 2], ub_ref.at[1, 2], loc_s.at[2]),
    )
    for copy in local_copies:
        copy.start()

    src = lax.broadcasted_iota(jnp.int32, (256, 256), 0)
    dst = lax.broadcasted_iota(jnp.int32, (256, 256), 1)
    dcol = dst % SX
    froms = (
        jnp.where(dcol == SX - 1, dst - (SX - 1), dst + 1),
        jnp.where(dcol == 0, dst + (SX - 1), dst - 1),
        jnp.where(dst >= 256 - SX, dst - (256 - SX), dst + SX),
        jnp.where(dst < SX, dst + (256 - SX), dst - SX),
    )
    for k in range(4):
        perm[:, 256 * k : 256 * (k + 1)] = jnp.where(src == froms[k], 1.0, 0.0).astype(BF16)

    lcol = lax.broadcasted_iota(jnp.int32, (18, 256), 1) % SX
    for z in range(2):
        links = lz_ref[z, 0]
        ub_ref[z, 0] = jnp.where(
            lcol == 0, pltpu.roll(links, 256 - (SX - 1), axis=1), pltpu.roll(links, 1, axis=1)
        )
        ub_ref[z, 1] = pltpu.roll(lz_ref[z, 1], SX, axis=1)

    @pl.loop(0, 12)
    def _(i):
        z, m = i // 6, i % 6
        block = v_ref[:, pl.ds(pl.multiple_of(i * 256, 256), 256)]
        out = jnp.dot(block, perm[...], preferred_element_type=F32).astype(BF16)
        for k in range(4):
            w_ref[z, k, :, pl.ds(pl.multiple_of(m * 256, 256), 256)] = out[
                :, 256 * k : 256 * (k + 1)
            ]

    def gradient(d):
        @pl.loop(0, 4)
        def _(q):
            z, h = q // 2, q % 2
            lanes = pl.ds(pl.multiple_of(h * 128, 128), 128)

            def part(m):
                return pl.ds(pl.multiple_of(m * 256 + h * 128, 128), 128)

            @pl.loop(0, 8)
            def _(kc):
                rows = pl.ds(pl.multiple_of(kc * 16, 16), 16)
                outs = []
                for side in range(2):
                    v = [w_ref[z, 2 * d + side, rows, part(m)].astype(F32) for m in range(6)]
                    l_ref = lz_ref if side == 0 else ub_ref
                    u = [
                        jnp.broadcast_to(l_ref[z, d, i : i + 1, lanes], (16, 128))
                        for i in range(18)
                    ]
                    for a in range(3):
                        re = im = None
                        for b in range(3):
                            if side == 0:
                                ur, ui = u[3 * a + b], u[9 + 3 * a + b]
                                t0 = ur * v[b] - ui * v[3 + b]
                                t1 = ur * v[3 + b] + ui * v[b]
                            else:
                                ur, ui = u[3 * b + a], u[9 + 3 * b + a]
                                t0 = ur * v[b] + ui * v[3 + b]
                                t1 = ur * v[3 + b] - ui * v[b]
                            re = t0 if re is None else re + t0
                            im = t1 if im is None else im + t1
                        outs.append((re, im))
                for a in range(3):
                    re = (0.5 * (outs[a][0] - outs[3 + a][0])).astype(BF16)
                    im = (0.5 * (outs[a][1] - outs[3 + a][1])).astype(BF16)
                    below = pl.ds(pl.multiple_of(128 + kc * 16, 16), 16)
                    g_ref[d, rows, part(z * 6 + a)] = re
                    g_ref[d, rows, part(z * 6 + 3 + a)] = im
                    g_ref[d, below, part(z * 6 + a)] = im
                    g_ref[d, below, part(z * 6 + 3 + a)] = -re

    s_ref[...] = jnp.zeros_like(s_ref)
    for n in range(ITERS - 1):
        if n > 0:
            prepare(n)
            for copy in t_copies(n):
                copy.start()
        local_hops()
        if n == 2:
            for copy in halo_copies:
                copy.wait()
            for copy in local_copies:
                copy.wait()
        gradient(n)
        for direction in range(2):
            c = n + 3 * direction
            own_copy(c, direction).wait()
            relay_copy(c, direction).start()
        for copy in t_copies(n):
            copy.wait()
        finish(n)

    sol_ref[...] = total[...]

    row = lax.broadcasted_iota(jnp.int32, (96, 48), 0)
    col = lax.broadcasted_iota(jnp.int32, (96, 48), 1)
    row_m, row_r, row_p, row_s = row // 16, (row // 8) % 2, (row // 4) % 2, row % 4
    col_r, col_s, col_m = col // 24, (col // 6) % 4, col % 6
    same = (row_r == col_r) & (row_s == col_s)
    want = jnp.where(row_p == 0, row_m, (row_m + 3) % 6)
    value = jnp.where((row_p == 1) & (row_m >= 3), -1.0, 1.0)
    pick = jnp.where(same & (want == col_m), value, 0.0).astype(BF16)
    flat = total[...]
    for z in range(2):
        rows = []
        for r in range(2):
            halves = [flat[:, 4 * h + 2 * r + z, :] for h in range(2)]
            rows.append(jnp.concatenate(halves, axis=1))
        spinors = jnp.concatenate(rows, axis=0).astype(BF16)
        placed = jnp.dot(pick, spinors, preferred_element_type=F32).astype(BF16)
        for m in range(6):
            s_ref[0:16, (z * 6 + m) * 256 : (z * 6 + m + 1) * 256] = placed[16 * m : 16 * m + 16]

    def c_copy(target, o):
        return remote(
            csend.at[target], crecv.at[o], c_ss.at[o], c_rs.at[o], (grp, ta, target)
        )

    def p_copy(target, o):
        return remote(
            psend.at[target], precv.at[o], p_ss.at[o], p_rs.at[o], (grp, ta, target)
        )

    lane3 = lax.broadcasted_iota(jnp.int32, (8, 8, 128), 2)

    def products(vectors_ref, first):
        for d in range(3):
            c = dot_nt(vectors_ref[...], g_ref[d]).astype(BF16)
            csend[pl.ds(first, 8), :, 256 * d : 256 * (d + 1)] = c.reshape(8, 16, 256)
        p = dot_nt(vectors_ref[...], s_ref[...]).reshape(8, 2, 8, 128)
        psend[pl.ds(first, 8)] = jnp.where(lane3 < 16, p[:, 0], pltpu.roll(p[:, 1], 16, axis=2))

        @pl.loop(0, 8)
        def _(i):
            target = first + i
            o = (target - me + n_xyz) % n_xyz

            @pl.when(o != 0)
            def _():
                c_copy(target, o).start()
                p_copy(target, o).start()

    products(v_ref, grp * 8)
    for direction in range(2):
        for c in range(3):
            relay_copy(c + 3 * direction, direction).wait()
    products(vo_ref, (1 - grp) * 8)

    @pl.loop(1, n_xyz)
    def _(o):
        target = (me + o) % n_xyz
        c_copy(target, o).wait()
        p_copy(target, o).wait()

    c_sum = csend[me].astype(F32)
    p_sum = psend[me]
    for o in range(1, n_xyz):
        c_sum = c_sum + crecv[o].astype(F32)
        p_sum = p_sum + precv[o]
    cor_ref[...] = c_sum * scale
    p_sum = p_sum * scale
    tall = jnp.concatenate([p_sum, pltpu.roll(p_sum, 112, axis=1)], axis=0)
    wide = jnp.concatenate([tall, jnp.zeros((112, 128), F32)], axis=0).T
    per_ref[0] = wide[0:8]
    per_ref[1] = wide[8:16]


def body(sizes, right_sides, gauge_links, eigenvectors, step_lengths):
    rs = right_sides.reshape(2, 24, 2, 2, 128)
    rs = rs.transpose(1, 3, 0, 2, 4).reshape(24, 8, 128)
    links = gauge_links.reshape(4, 18, 2, 256)
    lz = links.transpose(2, 0, 1, 3)
    u8 = links.reshape(72, 2, 2, 128).transpose(0, 2, 1, 3)[:, :, None]
    u8 = jnp.broadcast_to(u8, (72, 2, 2, 2, 128)).reshape(4, 2, 3, 3, 8, 128)
    v = eigenvectors.reshape(128, 6, 2, 256).transpose(0, 2, 1, 3).reshape(128, 3072)
    vmem = pl.BlockSpec(memory_space=pltpu.VMEM)
    n_it = ITERS - 1
    dma = pltpu.SemaphoreType.DMA
    sol, cor, per = pl.pallas_call(
        functools.partial(kernel, sizes),
        out_shape=(
            jax.ShapeDtypeStruct((24, 8, 128), F32),
            jax.ShapeDtypeStruct((16, 768), F32),
            jax.ShapeDtypeStruct((2, 8, 128), F32),
        ),
        in_specs=[pl.BlockSpec(memory_space=pltpu.SMEM), vmem, vmem, vmem, vmem],
        out_specs=(vmem, vmem, vmem),
        scratch_shapes=[
            pltpu.VMEM((24, 8, 128), F32),
            pltpu.VMEM((24, 8, 128), F32),
            pltpu.VMEM((24, 8, 128), F32),
            pltpu.VMEM((n_it, 2, 2, 2, 3, 8, 128), F32),
            pltpu.VMEM((n_it, 2, 2, 2, 3, 8, 128), F32),
            pltpu.VMEM((n_it, 2, 2, 3, 8, 128), F32),
            pltpu.VMEM((n_it, 2, 2, 3, 8, 128), F32),
            pltpu.VMEM((2, 6, 128, 1536), BF16),
            pltpu.VMEM((2, 3, 18, 256), F32),
            pltpu.VMEM((256, 1024), BF16),
            pltpu.VMEM((3, 256, 3072), BF16),
            pltpu.VMEM((128, 3072), BF16),
            pltpu.VMEM((6, 128, 512), BF16),
            pltpu.VMEM((128, 3072), BF16),
            pltpu.VMEM((16, 16, 768), BF16),
            pltpu.VMEM((16, 16, 768), BF16),
            pltpu.VMEM((16, 8, 128), F32),
            pltpu.VMEM((16, 8, 128), F32),
            dma((n_it, 2)), dma((n_it, 2)), dma((n_it, 2)), dma((n_it, 2)),
            dma((2,)), dma((2,)), dma(()), dma(()), dma((3,)),
            dma((6,)), dma((6,)), dma((6,)), dma((6,)),
            dma((16,)), dma((16,)), dma((16,)), dma((16,)),
        ],
        compiler_params=pltpu.CompilerParams(
            collective_id=0, has_side_effects=True, vmem_limit_bytes=56 * 1024 * 1024
        ),
    )(step_lengths, rs, u8, lz, v)
    sol = sol.reshape(24, 2, 2, 2, 128).transpose(2, 0, 3, 1, 4).reshape(right_sides.shape)
    cor = cor.reshape(1, 16, 3, 2, 128)
    per = per[:, :, :16].transpose(2, 0, 1)[None]
    return sol, cor, per


def solution(mesh):
    n_grp, n_ta, n_xyz = (mesh.shape[a] for a in ("grp", "ta", "xyz"))
    scale = 1.0 / math.sqrt(2 * n_xyz * 256)
    return jax.shard_map(
        functools.partial(body, (n_grp, n_ta, n_xyz, scale)),
        mesh=mesh,
        in_specs=(
            P("grp", None, "ta", "xyz", None),
            P(None, None, "ta", "xyz", None),
            P("ta", "grp", None, "xyz", None),
            P(),
        ),
        out_specs=(
            P("grp", None, "ta", "xyz", None),
            P("ta", "xyz", None, None, "grp"),
            P("ta", "xyz", "grp", None),
        ),
        check_vma=False,
    )
```

profile of v0, /device:TPU:1, one launch (start us, length us, event | category | flops | bytes accessed | tf_op | source)
XLA Modules:
  0.0 55.5 jit_solution(7069467983613244114)
XLA Ops:
  0.6 2.3 %copy.15 = bf16[1,128,6,2,256]{1,4,2,3,0:T(8,128)(2,1)S(1)} copy(bf16[1,128,6,2,256]{4,3,2,1,0:T(2,128)(2,1)} %param.6) | data formatting | bytes 1572864 | tf_op args[2]
  3.0 0.0 copy-start
  3.0 1.2 %copy.16.v_ref = bf16[128,3072]{1,0:T(8,128)(2,1)} copy(bf16[128,3072]{0,1:T(8,128)(2,1)S(1)} %bitcast.22) | data formatting | bytes 1572864 | tf_op jit(solution)/shard_map/reshape | solution.py:428
  4.2 0.0 copy-done
  4.2 0.2 reshape_reshape.3
  4.3 0.1 copy.13
  4.4 0.0 copy-start.1
  4.4 0.8 %broadcast_in_dim.4 = f32[72,2,2,2,128]{4,3,2,1,0:T(2,128)} broadcast(f32[72,2,2,128]{3,2,1,0:T(2,128)S(1)} %copy.13), dimensions={0,1,3,4} | broadcast | bytes 442368 | tf_op jit(solution)/shard_map/broadcast_in_dim | solution.py:427
  5.2 0.1 copy-done.1
  5.3 0.1 reshape.34
  5.4 0.7 %copy.12 = f32[2,24,2,2,128]{4,2,0,3,1:T(2,128)} copy(f32[2,24,2,2,128]{4,3,2,1,0:T(2,128)S(1)} %reshape.34) | data formatting | bytes 196608 | tf_op jit(solution)/shard_map/reshape | solution.py:422
  6.1 0.7 %copy.19 = f32[4,18,1,2,256]{4,1,0,3,2:T(8,128)} copy(f32[4,18,1,2,256]{4,3,2,1,0:T(2,128)S(1)} %copy-done) | data formatting | bytes 294912 | tf_op args[1]
  6.8 45.6 %shard_map.67 = (f32[24,8,128]{2,1,0:T(8,128)}, f32[16,768]{1,0:T(8,128)}, f32[2,8,128]{2,1,0:T(8,128)}) custom-call(f32[4]{0:T(128)} %al_ref.1, f32[24,8,128]{2,1,0:T(8,128)} %bitcast.26, f32[4,2,3,3,8,128]{5,4,3,2,1,0:T(8,128)} %bitcast.23, f32[2,4,18,256]{3,2,1,0:T(8,128)} %bitcast.24, bf16[128,3072]{1,0:T(8,128)(2,1)} %copy.16.v_ref), custom_call_target="tpu_custom_call" | custom-call | tf_op jit(solution)/shard_map/pallas_call | solution.py:432
  52.4 0.9 %copy.17 = f32[2,24,2,2,128]{4,3,2,1,0:T(2,128)S(1)} copy(f32[2,24,2,2,128]{4,2,0,3,1:T(2,128)} %bitcast.27) | data formatting | bytes 196608 | tf_op jit(solution)/shard_map/transpose | solution.py:469
  53.4 0.0 copy-start.2
  53.4 0.8 %reshape.41 = f32[2,24,1,2,256]{4,3,2,1,0:T(2,128)} reshape(f32[2,24,2,2,128]{4,3,2,1,0:T(2,128)S(1)} %copy.17) | data formatting | bytes 196608 | tf_op jit(solution)/shard_map/reshape | solution.py:469
  54.1 0.0 copy-done.2
  54.2 0.0 copy-start.3
  54.2 0.6 %reshape.42 = f32[1,16,3,2,128]{4,3,2,1,0:T(2,128)} reshape(f32[16,768]{1,0:T(8,128)S(1)} %copy-done.2) | data formatting | bytes 98304 | tf_op jit(solution)/shard_map/reshape | solution.py:470
  54.8 0.0 copy-done.3
  54.9 0.6 %slice_bitcast_fusion = f32[1,16,2,8]{1,3,2,0:T(8,128)} fusion(f32[2,8,128]{2,1,0:T(8,128)S(1)} %copy-done.3), kind=kLoop, calls=%fused_computation.1 | loop fusion | bytes 2048 | tf_op jit(solution)/shard_map/broadcast_in_dim | solution.py:471
Async XLA Ops:
  3.0 1.2 %copy-start = (f32[4,18,1,2,256]{4,3,2,1,0:T(2,128)S(1)}, f32[4,18,1,2,256]{4,3,2,1,0:T(2,128)}, u32[]{:S(2)}) copy-start(f32[4,18,1,2,256]{4,3,2,1,0:T(2,128)} %param.5) | copy-start | bytes 442372
  4.4 0.9 %copy-start.1 = (f32[2,24,1,2,256]{4,3,2,1,0:T(2,128)S(1)}, f32[2,24,1,2,256]{4,3,2,1,0:T(2,128)}, u32[]{:S(2)}) copy-start(f32[2,24,1,2,256]{4,3,2,1,0:T(2,128)} %param.4) | copy-start | bytes 294916
  53.4 0.8 %copy-start.2 = (f32[16,768]{1,0:T(8,128)S(1)}, f32[16,768]{1,0:T(8,128)}, u32[]{:S(2)}) copy-start(f32[16,768]{1,0:T(8,128)} %get-tuple-element.7) | copy-start | bytes 147460
  54.2 0.7 %copy-start.3 = (f32[2,8,128]{2,1,0:T(8,128)S(1)}, f32[2,8,128]{2,1,0:T(8,128)}, u32[]{:S(2)}) copy-start(f32[2,8,128]{2,1,0:T(8,128)} %get-tuple-element.8) | copy-start | bytes 24580
where the time goes:
time: 55.8 us; the launch traced here: 55.5 us
  Pallas kernels  45.6 us (82%)
  local copies, waits for them, and re-layouts  9.17 us (16%)
  between operations  0.69 us (1%)
    pallas_call x1, Pallas kernels, body(): pl.pallas_call(functools.partial(kernel, sizes), out_shape=(jax.ShapeDtyp...  45.6 us
    unnamed x10, local copies, waits for them, and re-layouts  3.22 us
    reshape x1, local copies, waits for them, and re-layouts, body(): eigenvectors.reshape(128, 6, 2, 256).transpose(0, 2, 1, 3)  1.17 us

commit v1 on v0

v1 whole, which is shorter than its diff:
```python
import functools
import math

import jax
import jax.numpy as jnp
from jax import lax
from jax.experimental import pallas as pl
from jax.experimental.pallas import tpu as pltpu
from jax.sharding import PartitionSpec as P

MESH = pl.DeviceIdType.MESH
F32 = jnp.float32
BF16 = jnp.bfloat16
SX = 16
ITERS = 4
HOPPING = 0.1
GAMMA_TABLE = (
    ((3, 0, 1), (2, 0, 1), (1, 0, -1), (0, 0, -1)),
    ((3, -1, 0), (2, 1, 0), (1, 1, 0), (0, -1, 0)),
    ((2, 0, 1), (3, 0, -1), (0, 0, -1), (1, 0, 1)),
    ((2, 1, 0), (3, 1, 0), (0, 1, 0), (1, 1, 0)),
)


def dot_nt(a, b):
    return lax.dot_general(a, b, (((1,), (1,)), ((), ())), preferred_element_type=F32)


def plus(a, b, sign):
    return a + b if sign > 0 else a - b


def phased(re, im, pr, pi):
    if pi == 0:
        return (pr, re), (pr, im)
    return (-pi, im), (pi, re)


def project(psi, direction, sign):
    re, im = [], []
    for target in range(2):
        source, pr, pi = GAMMA_TABLE[direction][target]
        (s0, a0), (s1, a1) = phased(psi[source][0], psi[source][1], pr, pi)
        re.append(plus(psi[target][0], a0, sign * s0))
        im.append(plus(psi[target][1], a1, sign * s1))
    return jnp.stack(re), jnp.stack(im)


def rebuild(acc, re, im, direction, sign):
    for target in range(4):
        if target < 2:
            terms = ((1, re[target]), (1, im[target]))
        else:
            source, pr, pi = GAMMA_TABLE[direction][target]
            (s0, a0), (s1, a1) = phased(re[source], im[source], pr, pi)
            terms = ((sign * s0, a0), (sign * s1, a1))
        for part in range(2):
            s, a = terms[part]
            old = acc[target][part]
            if old is None:
                acc[target][part] = a if s > 0 else -a
            else:
                acc[target][part] = plus(old, a, s)


def colour(u, re, im, dagger):
    out_re = out_im = None
    for b in range(3):
        ur = u[0, b] if dagger else u[0, :, b]
        ui = u[1, b] if dagger else u[1, :, b]
        vr, vi = re[:, b][:, None], im[:, b][:, None]
        ur, ui = ur[None], ui[None]
        t0 = plus(ur * vr, ui * vi, 1 if dagger else -1)
        t1 = plus(ur * vi, ui * vr, -1 if dagger else 1)
        out_re = t0 if out_re is None else out_re + t0
        out_im = t1 if out_im is None else out_im + t1
    return out_re, out_im


def roll(v, shift, axis):
    shape = v.shape
    flat = v.reshape((-1,) + shape[-2:])
    return pltpu.roll(flat, shift % shape[axis - 2 + len(shape)], axis=1 + axis).reshape(shape)


def kernel(
    sizes, al_ref, rs_hbm, lk_hbm, v_hbm,
    sol_ref, cor_ref, per_ref,
    rs_v, lk_v, vraw, v32, vall, relay, u8, lz, uz,
    res, total, hsum, tsend, trecv, zsend, zrecv, w_ref, ub_ref, perm, g_ref, s_ref,
    csend, crecv, psend, precv,
    t_ss, t_rs, z_ss, z_rs, vh_ss, vh_rs, uh_ss, uh_rs, loc_s,
    o_ss, o_rs, r_ss, r_rs, c_ss, c_rs, p_ss, p_rs,
):
    n_grp, n_ta, n_xyz, scale = sizes
    grp = lax.axis_index("grp")
    ta = lax.axis_index("ta")
    me = lax.axis_index("xyz")
    half_ta = n_ta // 2
    y = grp * 2 + ta // half_ta
    x = ta % half_ta

    def y_device(step):
        other = (y + step + 4) % 4
        return (other // 2, (other % 2) * half_ta + x, me)

    z_next = (grp, ta, (me + 1) % n_xyz)
    z_prev = (grp, ta, (me + n_xyz - 1) % n_xyz)
    t_next = (grp, (ta + 1) % n_ta, me)
    t_prev = (grp, (ta + n_ta - 1) % n_ta, me)

    barrier = pltpu.get_barrier_semaphore()
    for device in (y_device(1), y_device(-1), t_next, t_prev):
        pl.semaphore_signal(barrier, inc=1, device_id=device, device_id_type=MESH)

    @pl.loop(1, n_xyz)
    def _(o):
        pl.semaphore_signal(
            barrier, inc=1, device_id=(grp, ta, (me + o) % n_xyz), device_id_type=MESH
        )

    fetches = (
        pltpu.make_async_copy(lk_hbm, lk_v, loc_s.at[0]),
        pltpu.make_async_copy(rs_hbm, rs_v, loc_s.at[1]),
        pltpu.make_async_copy(v_hbm, vraw.at[0], loc_s.at[2]),
    )
    for copy in fetches:
        copy.start()

    def remote(src, dst, ss, rs, device):
        return pltpu.make_async_remote_copy(
            src_ref=src, dst_ref=dst, send_sem=ss, recv_sem=rs, device_id=device,
            device_id_type=MESH,
        )

    lane = lax.broadcasted_iota(jnp.int32, (8, 128), 1)
    sub = lax.broadcasted_iota(jnp.int32, (8, 128), 0)
    column = lane % SX
    z_is0 = sub % 2 == 0

    def shift_x(v, step):
        if step > 0:
            return jnp.where(column == SX - 1, roll(v, SX - 1, 1), roll(v, -1, 1))
        return jnp.where(column == 0, roll(v, 1 - SX, 1), roll(v, 1, 1))

    def shift_y(v, step):
        a = roll(v, -step * SX, 1)
        keep = lane < 128 - SX if step > 0 else lane >= SX
        return jnp.where(keep, a, roll(a, 4, 0))

    def spins(ref):
        v = ref[...].reshape(24, 8, 128)
        return [[v[6 * s + 3 * p : 6 * s + 3 * p + 3] for p in range(2)] for s in range(4)]

    def put(ref, s, p, value):
        k = 8 * (6 * s + 3 * p)
        ref[k : k + 24, :] = value.reshape(24, 128)

    def links_of(d):
        return u8[144 * d : 144 * (d + 1), :].reshape(2, 3, 3, 8, 128)

    def t_copies(n):
        return (
            remote(tsend.at[n, 0], trecv.at[n, 0], t_ss.at[n, 0], t_rs.at[n, 0], t_prev),
            remote(tsend.at[n, 1], trecv.at[n, 1], t_ss.at[n, 1], t_rs.at[n, 1], t_next),
            remote(zsend.at[n, 0], zrecv.at[n, 0], z_ss.at[n, 0], z_rs.at[n, 0], z_prev),
            remote(zsend.at[n, 1], zrecv.at[n, 1], z_ss.at[n, 1], z_rs.at[n, 1], z_next),
        )

    def prepare(n):
        psi = spins(res)
        re, im = project(psi, 3, -1)
        tsend[n, 0, 0], tsend[n, 0, 1] = re, im
        re, im = colour(links_of(3), *project(psi, 3, 1), True)
        tsend[n, 1, 0], tsend[n, 1, 1] = re, im
        re, im = project(psi, 2, -1)
        zsend[n, 0, 0] = jnp.where(z_is0, re[0], roll(re[1], 1, 0))
        zsend[n, 0, 1] = jnp.where(z_is0, im[0], roll(im[1], 1, 0))
        re, im = colour(links_of(2), *project(psi, 2, 1), True)
        zsend[n, 1, 0] = jnp.where(z_is0, roll(re[1], 7, 0), re[0])
        zsend[n, 1, 1] = jnp.where(z_is0, roll(im[1], 7, 0), im[0])

    def local_hops():
        psi = spins(res)
        acc = [[None, None] for _ in range(4)]
        for d, shift in ((0, shift_x), (1, shift_y)):
            re, im = project(psi, d, -1)
            rebuild(acc, *colour(links_of(d), shift(re, 1), shift(im, 1), False), d, -1)
            re, im = colour(links_of(d), *project(psi, d, 1), True)
            rebuild(acc, shift(re, -1), shift(im, -1), d, 1)
        for s in range(4):
            for p in range(2):
                put(hsum, s, p, acc[s][p])

    def finish(n):
        psi = spins(res)
        acc = spins(hsum)
        sums = spins(total)
        sign_up = jnp.where(ta == n_ta - 1, -1.0, 1.0).astype(F32)
        sign_down = jnp.where(ta == 0, -1.0, 1.0).astype(F32)
        re, im = project(psi, 2, -1)

        def ahead(v, got):
            return jnp.where(z_is0, roll(v, 7, 0), jnp.stack([roll(got, 1, 0), got]))

        re, im = ahead(re, zrecv[n, 0, 0]), ahead(im, zrecv[n, 0, 1])
        rebuild(acc, *colour(links_of(2), re, im, False), 2, -1)
        re, im = colour(links_of(2), *project(psi, 2, 1), True)

        def behind(v, got):
            return jnp.where(z_is0, jnp.stack([roll(got, 7, 0), got]), roll(v, 1, 0))

        re, im = behind(re, zrecv[n, 1, 0]), behind(im, zrecv[n, 1, 1])
        rebuild(acc, re, im, 2, 1)
        re, im = trecv[n, 0, 0] * sign_up, trecv[n, 0, 1] * sign_up
        rebuild(acc, *colour(links_of(3), re, im, False), 3, -1)
        rebuild(acc, trecv[n, 1, 0] * sign_down, trecv[n, 1, 1] * sign_down, 3, 1)
        step = al_ref[n]
        step_after = al_ref[n + 1]
        for s in range(4):
            for p in range(2):
                old = psi[s][p]
                new = old - step * (old - HOPPING * acc[s][p])
                put(res, s, p, new)
                put(total, s, p, sums[s][p] + step_after * new)

    src = lax.broadcasted_iota(jnp.int32, (256, 256), 0)
    dst = lax.broadcasted_iota(jnp.int32, (256, 256), 1)
    dcol = dst % SX
    froms = (
        jnp.where(dcol == SX - 1, dst - (SX - 1), dst + 1),
        jnp.where(dcol == 0, dst + (SX - 1), dst - 1),
        jnp.where(dst >= 256 - SX, dst - (256 - SX), dst + SX),
        jnp.where(dst < SX, dst + (256 - SX), dst - SX),
    )
    for k in range(4):
        perm[:, 256 * k : 256 * (k + 1)] = jnp.where(src == froms[k], 1.0, 0.0).astype(BF16)
    s_ref[...] = jnp.zeros_like(s_ref)

    fetches[0].wait()
    fetches[1].wait()
    first_step = al_ref[0]
    for h in range(2):
        for z in range(2):
            links = lk_v[pl.ds(2 * h + z, 72, stride=4), :]
            for r in range(2):
                u8[pl.ds(4 * h + 2 * r + z, 72, stride=8), :] = links
                values = rs_v[pl.ds(96 * r + 2 * h + z, 24, stride=4), :]
                res[pl.ds(4 * h + 2 * r + z, 24, stride=8), :] = values
                total[pl.ds(4 * h + 2 * r + z, 24, stride=8), :] = first_step * values
            for d in range(3):
                rows = lk_v[pl.ds(72 * d + 2 * h + z, 18, stride=4), :]
                lz[z, d, :, 128 * h : 128 * (h + 1)] = rows
                if d == 2 and z == 1:
                    uz[:, 128 * h : 128 * (h + 1)] = rows
                if d == 2 and z == 0:
                    ub_ref[1, 2, :, 128 * h : 128 * (h + 1)] = rows
    lcol = lax.broadcasted_iota(jnp.int32, (18, 256), 1) % SX
    for z in range(2):
        links = lz[z, 0]
        ub_ref[z, 0] = jnp.where(
            lcol == 0, pltpu.roll(links, 256 - (SX - 1), axis=1), pltpu.roll(links, 1, axis=1)
        )
        ub_ref[z, 1] = pltpu.roll(lz[z, 1], SX, axis=1)

    pl.semaphore_wait(barrier, n_xyz - 1 + 4)

    def way(c):
        return y_device(1 - 2 * ((c // 2) % 2))

    def own_copy(c):
        rows = pl.ds(pl.multiple_of(c * 384, 384), 384)
        return remote(v_hbm.at[rows], relay.at[c], o_ss.at[c], o_rs.at[c], way(c))

    def relay_copy(c):
        rows = pl.ds(pl.multiple_of(c * 384, 384), 384)
        return remote(relay.at[c], vraw.at[1, rows], r_ss.at[c], r_rs.at[c], way(c))

    def pass_on(step):
        for c in (step + 2 * (step // 2), step + 2 * (step // 2) + 2):
            own_copy(c).wait()
            relay_copy(c).start()

    def sort_chunk(which, c):
        v32[...] = vraw[which, pl.ds(pl.multiple_of(c * 384, 384), 384), :].astype(F32)
        rows = pl.ds(pl.multiple_of(c * 16, 16), 16)
        for m in range(6):
            for h in range(2):
                for z in range(2):
                    k = (z * 6 + m) * 256 + h * 128
                    vall[which, rows, k : k + 128] = v32[
                        pl.ds(4 * m + 2 * h + z, 16, stride=24), :
                    ].astype(BF16)

    low, high = vall.at[0, :, pl.ds(0, 1536)], vall.at[0, :, pl.ds(1536, 1536)]
    halo_copies = (
        remote(low, w_ref.at[1, 4], vh_ss.at[0], vh_rs.at[0], z_prev),
        remote(high, w_ref.at[0, 5], vh_ss.at[1], vh_rs.at[1], z_next),
        remote(uz, ub_ref.at[0, 2], uh_ss, uh_rs, z_next),
        pltpu.make_async_copy(high, w_ref.at[0, 4], loc_s.at[0]),
        pltpu.make_async_copy(low, w_ref.at[1, 5], loc_s.at[1]),
    )

    def gradient(d):
        @pl.loop(0, 4)
        def _(q):
            z, h = q // 2, q % 2
            lanes = pl.ds(pl.multiple_of(h * 128, 128), 128)

            def part(m):
                return pl.ds(pl.multiple_of(m * 256 + h * 128, 128), 128)

            @pl.loop(0, 8)
            def _(kc):
                rows = pl.ds(pl.multiple_of(kc * 16, 16), 16)
                outs = []
                for side in range(2):
                    v = [w_ref[z, 2 * d + side, rows, part(m)].astype(F32) for m in range(6)]
                    l_ref = lz if side == 0 else ub_ref
                    u = [
                        jnp.broadcast_to(l_ref[z, d, i : i + 1, lanes], (16, 128))
                        for i in range(18)
                    ]
                    for a in range(3):
                        re = im = None
                        for b in range(3):
                            if side == 0:
                                ur, ui = u[3 * a + b], u[9 + 3 * a + b]
                                t0 = ur * v[b] - ui * v[3 + b]
                                t1 = ur * v[3 + b] + ui * v[b]
                            else:
                                ur, ui = u[3 * b + a], u[9 + 3 * b + a]
                                t0 = ur * v[b] + ui * v[3 + b]
                                t1 = ur * v[3 + b] - ui * v[b]
                            re = t0 if re is None else re + t0
                            im = t1 if im is None else im + t1
                        outs.append((re, im))
                for a in range(3):
                    re = (0.5 * (outs[a][0] - outs[3 + a][0])).astype(BF16)
                    im = (0.5 * (outs[a][1] - outs[3 + a][1])).astype(BF16)
                    above = pl.ds(pl.multiple_of(d * 256 + kc * 16, 16), 16)
                    below = pl.ds(pl.multiple_of(d * 256 + 128 + kc * 16, 16), 16)
                    g_ref[above, part(z * 6 + a)] = re
                    g_ref[above, part(z * 6 + 3 + a)] = im
                    g_ref[below, part(z * 6 + a)] = im
                    g_ref[below, part(z * 6 + 3 + a)] = -re

    @pl.loop(0, ITERS - 1)
    def _(n):
        prepare(n)
        for copy in t_copies(n):
            copy.start()

        @pl.when(n == 0)
        def _():
            @pl.loop(0, 8)
            def _(i):
                own_copy(i // 4 * 4 + (i % 2) * 2 + (i // 2) % 2).start()

        local_hops()

        @pl.when(n == 0)
        def _():
            fetches[2].wait()

            @pl.loop(0, 8)
            def _(c):
                sort_chunk(0, c)

            for copy in halo_copies:
                copy.start()

            @pl.loop(0, 12)
            def _(i):
                z, m = i // 6, i % 6
                block = vall[0, :, pl.ds(pl.multiple_of(i * 256, 256), 256)]
                out = jnp.dot(block, perm[...], preferred_element_type=F32).astype(BF16)
                for k in range(4):
                    w_ref[z, k, :, pl.ds(pl.multiple_of(m * 256, 256), 256)] = out[
                        :, 256 * k : 256 * (k + 1)
                    ]

        @pl.when(n == 2)
        def _():
            for copy in halo_copies:
                copy.wait()

        gradient(n)
        pass_on(n)
        for copy in t_copies(n):
            copy.wait()
        finish(n)

    pass_on(3)

    row = lax.broadcasted_iota(jnp.int32, (96, 48), 0)
    col = lax.broadcasted_iota(jnp.int32, (96, 48), 1)
    row_m, row_r, row_p, row_s = row // 16, (row // 8) % 2, (row // 4) % 2, row % 4
    col_r, col_s, col_m = col // 24, (col // 6) % 4, col % 6
    same = (row_r == col_r) & (row_s == col_s)
    want = jnp.where(row_p == 0, row_m, (row_m + 3) % 6)
    value = jnp.where((row_p == 1) & (row_m >= 3), -1.0, 1.0)
    pick = jnp.where(same & (want == col_m), value, 0.0).astype(BF16)
    for z in range(2):
        rows = []
        for r in range(2):
            halves = []
            for h in range(2):
                values = total[pl.ds(4 * h + 2 * r + z, 24, stride=8), :]
                sol_ref[pl.ds(96 * r + 2 * h + z, 24, stride=4), :] = values
                halves.append(values)
            rows.append(jnp.concatenate(halves, axis=1))
        spinors = jnp.concatenate(rows, axis=0).astype(BF16)
        placed = jnp.dot(pick, spinors, preferred_element_type=F32).astype(BF16)
        for m in range(6):
            s_ref[0:16, (z * 6 + m) * 256 : (z * 6 + m + 1) * 256] = placed[16 * m : 16 * m + 16]

    def c_copy(target, o):
        return remote(
            csend.at[target], crecv.at[o], c_ss.at[o], c_rs.at[o], (grp, ta, target)
        )

    def p_copy(target, o):
        return remote(
            psend.at[target], precv.at[o], p_ss.at[o], p_rs.at[o], (grp, ta, target)
        )

    lane3 = lax.broadcasted_iota(jnp.int32, (4, 8, 128), 2)

    @pl.loop(0, 4)
    def _(phase):
        which, half = phase // 2, phase % 2

        @pl.when(which == 1)
        def _():
            @pl.loop(0, 4)
            def _(j):
                relay_copy(4 * half + j).wait()
                sort_chunk(1, 4 * half + j)

        first = (grp + which - 2 * grp * which) * 8 + half * 4
        rows = pl.ds(pl.multiple_of(half * 64, 64), 64)

        @pl.loop(0, 3)
        def _(d):
            block = pl.ds(pl.multiple_of(d * 256, 256), 256)
            c = dot_nt(g_ref[block, :], vall[which, rows, :]).T.astype(BF16)
            csend[pl.ds(first, 4), :, block] = c.reshape(4, 16, 256)

        p = dot_nt(s_ref[...], vall[which, rows, :]).T.reshape(4, 2, 8, 128)
        psend[pl.ds(first, 4)] = jnp.where(lane3 < 16, p[:, 0], pltpu.roll(p[:, 1], 16, axis=2))

        @pl.loop(0, 4)
        def _(i):
            target = first + i
            o = (target - me + n_xyz) % n_xyz

            @pl.when(o != 0)
            def _():
                c_copy(target, o).start()
                p_copy(target, o).start()

    @pl.loop(1, n_xyz)
    def _(o):
        target = (me + o) % n_xyz
        c_copy(target, o).wait()
        p_copy(target, o).wait()

    c_sum = csend[me].astype(F32)
    p_sum = psend[me]
    for o in range(1, n_xyz):
        c_sum = c_sum + crecv[o].astype(F32)
        p_sum = p_sum + precv[o]
    for k in range(6):
        cor_ref[pl.ds(k, 16, stride=6), :] = c_sum[:, 128 * k : 128 * (k + 1)] * scale
    p_sum = p_sum * scale
    tall = jnp.concatenate([p_sum, pltpu.roll(p_sum, 112, axis=1)], axis=0)
    wide = jnp.concatenate([tall, jnp.zeros((112, 128), F32)], axis=0).T
    per_ref[0] = wide[0:8, 0:16]
    per_ref[1] = wide[8:16, 0:16]


def rows_of(array, lead):
    return array.reshape(lead, 2, 2, 128).transpose(0, 2, 1, 3).reshape(lead * 4, 128)


def body(sizes, right_sides, gauge_links, eigenvectors, step_lengths):
    vmem = pl.BlockSpec(memory_space=pltpu.VMEM)
    anywhere = pl.BlockSpec(memory_space=pl.ANY)
    n_it = ITERS - 1
    dma = pltpu.SemaphoreType.DMA
    sol, cor, per = pl.pallas_call(
        functools.partial(kernel, sizes),
        out_shape=(
            jax.ShapeDtypeStruct((192, 128), F32),
            jax.ShapeDtypeStruct((96, 128), F32),
            jax.ShapeDtypeStruct((2, 8, 16), F32),
        ),
        in_specs=[pl.BlockSpec(memory_space=pltpu.SMEM), anywhere, anywhere, anywhere],
        out_specs=(vmem, vmem, vmem),
        scratch_shapes=[
            pltpu.VMEM((192, 128), F32),
            pltpu.VMEM((288, 128), F32),
            pltpu.VMEM((2, 3072, 128), BF16),
            pltpu.VMEM((384, 128), F32),
            pltpu.VMEM((2, 128, 3072), BF16),
            pltpu.VMEM((8, 384, 128), BF16),
            pltpu.VMEM((576, 128), F32),
            pltpu.VMEM((2, 3, 18, 256), F32),
            pltpu.VMEM((18, 256), F32),
            pltpu.VMEM((192, 128), F32),
            pltpu.VMEM((192, 128), F32),
            pltpu.VMEM((192, 128), F32),
            pltpu.VMEM((n_it, 2, 2, 2, 3, 8, 128), F32),
            pltpu.VMEM((n_it, 2, 2, 2, 3, 8, 128), F32),
            pltpu.VMEM((n_it, 2, 2, 3, 8, 128), F32),
            pltpu.VMEM((n_it, 2, 2, 3, 8, 128), F32),
            pltpu.VMEM((2, 6, 128, 1536), BF16),
            pltpu.VMEM((2, 3, 18, 256), F32),
            pltpu.VMEM((256, 1024), BF16),
            pltpu.VMEM((768, 3072), BF16),
            pltpu.VMEM((128, 3072), BF16),
            pltpu.VMEM((16, 16, 768), BF16),
            pltpu.VMEM((16, 16, 768), BF16),
            pltpu.VMEM((16, 8, 128), F32),
            pltpu.VMEM((16, 8, 128), F32),
            dma((n_it, 2)), dma((n_it, 2)), dma((n_it, 2)), dma((n_it, 2)),
            dma((2,)), dma((2,)), dma(()), dma(()), dma((3,)),
            dma((8,)), dma((8,)), dma((8,)), dma((8,)),
            dma((16,)), dma((16,)), dma((16,)), dma((16,)),
        ],
        compiler_params=pltpu.CompilerParams(
            collective_id=0, has_side_effects=True, vmem_limit_bytes=56 * 1024 * 1024
        ),
    )(
        step_lengths,
        rows_of(right_sides, 48),
        rows_of(gauge_links, 72),
        rows_of(eigenvectors, 768),
    )
    sol = sol.reshape(48, 2, 2, 128).transpose(0, 2, 1, 3).reshape(right_sides.shape)
    cor = cor.reshape(1, 16, 3, 2, 128)
    return sol, cor, per.transpose(2, 0, 1)[None]


def solution(mesh):
    n_grp, n_ta, n_xyz = (mesh.shape[a] for a in ("grp", "ta", "xyz"))
    scale = 1.0 / math.sqrt(2 * n_xyz * 256)
    return jax.shard_map(
        functools.partial(body, (n_grp, n_ta, n_xyz, scale)),
        mesh=mesh,
        in_specs=(
            P("grp", None, "ta", "xyz", None),
            P(None, None, "ta", "xyz", None),
            P("ta", "grp", None, "xyz", None),
            P(),
        ),
        out_specs=(
            P("grp", None, "ta", "xyz", None),
            P("ta", "xyz", None, None, "grp"),
            P("ta", "xyz", "grp", None),
        ),
        check_vma=False,
    )
```

time: 55.8 us -> 47.6 us (0.85)
  the two profiles are of different devices: /device:TPU:1 before, /device:TPU:81 now
where the time goes in v1:
time: 47.6 us; the launch traced here: 47.4 us
  Pallas kernels  43.9 us (92%)
  local copies, waits for them, and re-layouts  2.85 us (6%)
  between operations  0.65 us (1%)
    pallas_call x1, Pallas kernels, body(): pl.pallas_call(functools.partial(kernel, sizes), out_shape=(jax.ShapeDtyp...  43.9 us
    unnamed x7, local copies, waits for them, and re-layouts  2.85 us

profile of v1, /device:TPU:81, one launch (start us, length us, event | category | flops | bytes accessed | tf_op | source)
XLA Modules:
  0.0 47.4 jit_solution(10320128333672047796)
XLA Ops:
  0.6 43.9 %shard_map.67 = (f32[192,128]{1,0:T(8,128)}, f32[96,128]{1,0:T(8,128)}, f32[2,8,16]{2,1,0:T(8,128)}) custom-call(f32[4]{0:T(128)} %al_ref.1, f32[192,128]{1,0:T(8,128)} %bitcast.26, f32[288,128]{1,0:T(8,128)} %bitcast.25, bf16[3072,128]{1,0:T(8,128)(2,1)} %bitcast.24), custom_call_target="tpu_custom_call" | custom-call | tf_op jit(solution)/shard_map/pallas_call | solution.py:492
  44.6 0.0 copy-start
  44.6 1.6 %copy.14 = f32[2,24,1,2,256]{4,3,2,1,0:T(2,128)} copy(f32[2,24,1,2,256]{4,3,2,1,0:T(2,128)} %bitcast.27) | data formatting | bytes 196608
  46.1 0.0 copy-done
  46.1 0.0 copy-start.1
  46.1 0.6 %copy.15 = f32[1,16,3,2,128]{4,3,2,1,0:T(2,128)} copy(f32[1,16,3,2,128]{4,3,2,1,0:T(2,128)S(1)} %bitcast.28) | data formatting | bytes 98304
  46.8 0.1 copy-done.1
  46.8 0.6 %copy.16 = f32[1,16,2,8]{1,3,2,0:T(8,128)} copy(f32[1,16,2,8]{1,3,2,0:T(8,128)S(1)} %bitcast.29) | data formatting | bytes 2048
Async XLA Ops:
  44.6 1.6 %copy-start = (f32[96,128]{1,0:T(8,128)S(1)}, f32[96,128]{1,0:T(8,128)}, u32[]{:S(2)}) copy-start(f32[96,128]{1,0:T(8,128)} %get-tuple-element.7) | copy-start | bytes 147460
  46.1 0.7 %copy-start.1 = (f32[2,8,16]{2,1,0:T(8,128)S(1)}, f32[2,8,16]{2,1,0:T(8,128)}, u32[]{:S(2)}) copy-start(f32[2,8,16]{2,1,0:T(8,128)} %get-tuple-element.8) | copy-start | bytes 3076

commit v2 on v1

--- a/solution.py
+++ b/solution.py
@@ -87,7 +87,7 @@
     sizes, al_ref, rs_hbm, lk_hbm, v_hbm,
     sol_ref, cor_ref, per_ref,
     rs_v, lk_v, vraw, v32, vall, relay, u8, lz, uz,
-    res, total, hsum, tsend, trecv, zsend, zrecv, w_ref, ub_ref, perm, g_ref, s_ref,
+    res, total, hsum, tsend, trecv, zsend, zrecv, w_ref, ub_ref, g_ref, s_ref,
     csend, crecv, psend, precv,
     t_ss, t_rs, z_ss, z_rs, vh_ss, vh_rs, uh_ss, uh_rs, loc_s,
     o_ss, o_rs, r_ss, r_rs, c_ss, c_rs, p_ss, p_rs,
@@ -132,6 +132,17 @@
             src_ref=src, dst_ref=dst, send_sem=ss, recv_sem=rs, device_id=device,
             device_id_type=MESH,
         )
+
+    def way(c):
+        return y_device(1 - 2 * ((c // 2) % 2))
+
+    def own_copy(c):
+        rows = pl.ds(pl.multiple_of(c * 384, 384), 384)
+        return remote(v_hbm.at[rows], relay.at[c], o_ss.at[c], o_rs.at[c], way(c))
+
+    pl.semaphore_wait(barrier, n_xyz - 1 + 4)
+    own_copy(0).start()
+    own_copy(2).start()
 
     lane = lax.broadcasted_iota(jnp.int32, (8, 128), 1)
     sub = lax.broadcasted_iota(jnp.int32, (8, 128), 0)
@@ -224,19 +235,6 @@
                 put(res, s, p, new)
                 put(total, s, p, sums[s][p] + step_after * new)
 
-    src = lax.broadcasted_iota(jnp.int32, (256, 256), 0)
-    dst = lax.broadcasted_iota(jnp.int32, (256, 256), 1)
-    dcol = dst % SX
-    froms = (
-        jnp.where(dcol == SX - 1, dst - (SX - 1), dst + 1),
-        jnp.where(dcol == 0, dst + (SX - 1), dst - 1),
-        jnp.where(dst >= 256 - SX, dst - (256 - SX), dst + SX),
-        jnp.where(dst < SX, dst + (256 - SX), dst - SX),
-    )
-    for k in range(4):
-        perm[:, 256 * k : 256 * (k + 1)] = jnp.where(src == froms[k], 1.0, 0.0).astype(BF16)
-    s_ref[...] = jnp.zeros_like(s_ref)
-
     fetches[0].wait()
     fetches[1].wait()
     first_step = al_ref[0]
@@ -249,7 +247,7 @@
                 res[pl.ds(4 * h + 2 * r + z, 24, stride=8), :] = values
                 total[pl.ds(4 * h + 2 * r + z, 24, stride=8), :] = first_step * values
             for d in range(3):
-                rows = lk_v[pl.ds(72 * d + 2 * h + z, 18, stride=4), :]
+                rows = 0.5 * lk_v[pl.ds(72 * d + 2 * h + z, 18, stride=4), :]
                 lz[z, d, :, 128 * h : 128 * (h + 1)] = rows
                 if d == 2 and z == 1:
                     uz[:, 128 * h : 128 * (h + 1)] = rows
@@ -263,15 +261,6 @@
         )
         ub_ref[z, 1] = pltpu.roll(lz[z, 1], SX, axis=1)
 
-    pl.semaphore_wait(barrier, n_xyz - 1 + 4)
-
-    def way(c):
-        return y_device(1 - 2 * ((c // 2) % 2))
-
-    def own_copy(c):
-        rows = pl.ds(pl.multiple_of(c * 384, 384), 384)
-        return remote(v_hbm.at[rows], relay.at[c], o_ss.at[c], o_rs.at[c], way(c))
-
     def relay_copy(c):
         rows = pl.ds(pl.multiple_of(c * 384, 384), 384)
         return remote(relay.at[c], vraw.at[1, rows], r_ss.at[c], r_rs.at[c], way(c))
@@ -294,11 +283,11 @@
 
     low, high = vall.at[0, :, pl.ds(0, 1536)], vall.at[0, :, pl.ds(1536, 1536)]
     halo_copies = (
-        remote(low, w_ref.at[1, 4], vh_ss.at[0], vh_rs.at[0], z_prev),
-        remote(high, w_ref.at[0, 5], vh_ss.at[1], vh_rs.at[1], z_next),
+        remote(low, w_ref.at[1, 0], vh_ss.at[0], vh_rs.at[0], z_prev),
+        remote(high, w_ref.at[0, 1], vh_ss.at[1], vh_rs.at[1], z_next),
         remote(uz, ub_ref.at[0, 2], uh_ss, uh_rs, z_next),
-        pltpu.make_async_copy(high, w_ref.at[0, 4], loc_s.at[0]),
-        pltpu.make_async_copy(low, w_ref.at[1, 5], loc_s.at[1]),
+        pltpu.make_async_copy(high, w_ref.at[0, 0], loc_s.at[0]),
+        pltpu.make_async_copy(low, w_ref.at[1, 1], loc_s.at[1]),
     )
 
     def gradient(d):
@@ -306,16 +295,55 @@
         def _(q):
             z, h = q // 2, q % 2
             lanes = pl.ds(pl.multiple_of(h * 128, 128), 128)
-
-            def part(m):
-                return pl.ds(pl.multiple_of(m * 256 + h * 128, 128), 128)
-
-            @pl.loop(0, 8)
+            lane16 = lax.broadcasted_iota(jnp.int32, (16, 128), 1)
+
+            def part(m, side=h):
+                return pl.ds(pl.multiple_of(m * 256 + side * 128, 128), 128)
+
+            @pl.loop(0, 8, unroll=4)
             def _(kc):
                 rows = pl.ds(pl.multiple_of(kc * 16, 16), 16)
+
+                def own(m, side):
+                    return vall[0, rows, part(z * 6 + m, side)]
+
+                def neighbours(m):
+                    if d == 0:
+                        v = own(m, h)
+                        column = lane16 % SX
+                        return (
+                            jnp.where(
+                                column == SX - 1,
+                                pltpu.roll(v, SX - 1, axis=1),
+                                pltpu.roll(v, 127, axis=1),
+                            ),
+                            jnp.where(
+                                column == 0,
+                                pltpu.roll(v, 129 - SX, axis=1),
+                                pltpu.roll(v, 1, axis=1),
+                            ),
+                        )
+                    if d == 1:
+                        v, w = own(m, h), own(m, 1 - h)
+                        up, down = 128 - SX, SX
+                        return (
+                            jnp.where(
+                                lane16 < up,
+                                pltpu.roll(v, up, axis=1),
+                                pltpu.roll(w, up, axis=1),
+                            ),
+                            jnp.where(
+                                lane16 >= down,
+                                pltpu.roll(v, down, axis=1),
+                                pltpu.roll(w, down, axis=1),
+                            ),
+                        )
+                    return tuple(w_ref[z, s, rows, part(m)] for s in range(2))
+
+                both = [neighbours(m) for m in range(6)]
                 outs = []
                 for side in range(2):
-                    v = [w_ref[z, 2 * d + side, rows, part(m)].astype(F32) for m in range(6)]
+                    v = [both[m][side].astype(F32) for m in range(6)]
                     l_ref = lz if side == 0 else ub_ref
                     u = [
                         jnp.broadcast_to(l_ref[z, d, i : i + 1, lanes], (16, 128))
@@ -335,15 +363,50 @@
                             re = t0 if re is None else re + t0
                             im = t1 if im is None else im + t1
                         outs.append((re, im))
+                above = pl.ds(pl.multiple_of(d * 256 + kc * 16, 16), 16)
+                below = pl.ds(pl.multiple_of(d * 256 + 128 + kc * 16, 16), 16)
                 for a in range(3):
-                    re = (0.5 * (outs[a][0] - outs[3 + a][0])).astype(BF16)
-                    im = (0.5 * (outs[a][1] - outs[3 + a][1])).astype(BF16)
-                    above = pl.ds(pl.multiple_of(d * 256 + kc * 16, 16), 16)
-                    below = pl.ds(pl.multiple_of(d * 256 + 128 + kc * 16, 16), 16)
+                    re = (outs[a][0] - outs[3 + a][0]).astype(BF16)
+                    im = (outs[a][1] - outs[3 + a][1]).astype(BF16)
                     g_ref[above, part(z * 6 + a)] = re
                     g_ref[above, part(z * 6 + 3 + a)] = im
                     g_ref[below, part(z * 6 + a)] = im
                     g_ref[below, part(z * 6 + 3 + a)] = -re
+
+    def c_copy(target, o):
+        return remote(
+            csend.at[target], crecv.at[o], c_ss.at[o], c_rs.at[o], (grp, ta, target)
+        )
+
+    def p_copy(target, o):
+        return remote(
+            psend.at[target], precv.at[o], p_ss.at[o], p_rs.at[o], (grp, ta, target)
+        )
+
+    def send(copy_of, first, count):
+        @pl.loop(0, count)
+        def _(i):
+            target = first + i
+            o = (target - me + n_xyz) % n_xyz
+
+            @pl.when(o != 0)
+            def _():
+                copy_of(target, o).start()
+
+    def correlate(vectors, first):
+        count = vectors.shape[0] // 16
+        for d in range(3):
+            c = dot_nt(g_ref[256 * d : 256 * (d + 1), :], vectors).T.astype(BF16)
+            csend[pl.ds(first, count), :, 256 * d : 256 * (d + 1)] = c.reshape(count, 16, 256)
+        send(c_copy, first, count)
+
+    def overlap(vectors, first):
+        count = vectors.shape[0] // 16
+        p = dot_nt(vectors, s_ref[...]).reshape(2 * count, 8, 128)
+        p = jnp.where((lane // 16 == sub)[None], p, 0.0)
+        p = jnp.sum(p, axis=1, keepdims=True)
+        psend[pl.ds(first, count)] = p.reshape(count, 2, 1, 128)
+        send(p_copy, first, count)
 
     @pl.loop(0, ITERS - 1)
     def _(n):
@@ -353,7 +416,7 @@
 
         @pl.when(n == 0)
         def _():
-            @pl.loop(0, 8)
+            @pl.loop(2, 8)
             def _(i):
                 own_copy(i // 4 * 4 + (i % 2) * 2 + (i // 2) % 2).start()
 
@@ -370,22 +433,19 @@
             for copy in halo_copies:
                 copy.start()
 
-            @pl.loop(0, 12)
-            def _(i):
-                z, m = i // 6, i % 6
-                block = vall[0, :, pl.ds(pl.multiple_of(i * 256, 256), 256)]
-                out = jnp.dot(block, perm[...], preferred_element_type=F32).astype(BF16)
-                for k in range(4):
-                    w_ref[z, k, :, pl.ds(pl.multiple_of(m * 256, 256), 256)] = out[
-                        :, 256 * k : 256 * (k + 1)
-                    ]
+            gradient(0)
+
+        @pl.when(n == 1)
+        def _():
+            gradient(1)
 
         @pl.when(n == 2)
         def _():
             for copy in halo_copies:
                 copy.wait()
-
-        gradient(n)
+            gradient(2)
+            correlate(vall[0], grp * 8)
+
         pass_on(n)
         for copy in t_copies(n):
             copy.wait()
@@ -406,59 +466,31 @@
         for r in range(2):
             halves = []
             for h in range(2):
-                values = total[pl.ds(4 * h + 2 * r + z, 24, stride=8), :]
-                sol_ref[pl.ds(96 * r + 2 * h + z, 24, stride=4), :] = values
+                here = pl.ds(4 * h + 2 * r + z, 24, stride=8)
+                there = pl.ds(96 * r + 2 * h + z, 24, stride=4)
+                values = total[here, :]
+                sol_ref[there, :] = values
                 halves.append(values)
             rows.append(jnp.concatenate(halves, axis=1))
         spinors = jnp.concatenate(rows, axis=0).astype(BF16)
         placed = jnp.dot(pick, spinors, preferred_element_type=F32).astype(BF16)
         for m in range(6):
-            s_ref[0:16, (z * 6 + m) * 256 : (z * 6 + m + 1) * 256] = placed[16 * m : 16 * m + 16]
-
-    def c_copy(target, o):
-        return remote(
-            csend.at[target], crecv.at[o], c_ss.at[o], c_rs.at[o], (grp, ta, target)
-        )
-
-    def p_copy(target, o):
-        return remote(
-            psend.at[target], precv.at[o], p_ss.at[o], p_rs.at[o], (grp, ta, target)
-        )
-
-    lane3 = lax.broadcasted_iota(jnp.int32, (4, 8, 128), 2)
-
-    @pl.loop(0, 4)
-    def _(phase):
-        which, half = phase // 2, phase % 2
-
-        @pl.when(which == 1)
-        def _():
-            @pl.loop(0, 4)
-            def _(j):
-                relay_copy(4 * half + j).wait()
-                sort_chunk(1, 4 * half + j)
-
-        first = (grp + which - 2 * grp * which) * 8 + half * 4
-        rows = pl.ds(pl.multiple_of(half * 64, 64), 64)
-
-        @pl.loop(0, 3)
-        def _(d):
-            block = pl.ds(pl.multiple_of(d * 256, 256), 256)
-            c = dot_nt(g_ref[block, :], vall[which, rows, :]).T.astype(BF16)
-            csend[pl.ds(first, 4), :, block] = c.reshape(4, 16, 256)
-
-        p = dot_nt(s_ref[...], vall[which, rows, :]).T.reshape(4, 2, 8, 128)
-        psend[pl.ds(first, 4)] = jnp.where(lane3 < 16, p[:, 0], pltpu.roll(p[:, 1], 16, axis=2))
-
+            rows = placed[16 * m : 16 * m + 16]
+            s_ref[:, (z * 6 + m) * 256 : (z * 6 + m + 1) * 256] = jnp.concatenate([rows] * 8)
+
+    overlap(vall[0], grp * 8)
+
+    @pl.loop(0, 2)
+    def _(half):
         @pl.loop(0, 4)
-        def _(i):
-            target = first + i
-            o = (target - me + n_xyz) % n_xyz
-
-            @pl.when(o != 0)
-            def _():
-                c_copy(target, o).start()
-                p_copy(target, o).start()
+        def _(j):
+            relay_copy(4 * half + j).wait()
+            sort_chunk(1, 4 * half + j)
+
+        first = (1 - grp) * 8 + half * 4
+        vectors = vall[1, pl.ds(pl.multiple_of(half * 64, 64), 64), :]
+        correlate(vectors, first)
+        overlap(vectors, first)
 
     @pl.loop(1, n_xyz)
     def _(o):
@@ -474,8 +506,14 @@
     for k in range(6):
         cor_ref[pl.ds(k, 16, stride=6), :] = c_sum[:, 128 * k : 128 * (k + 1)] * scale
     p_sum = p_sum * scale
-    tall = jnp.concatenate([p_sum, pltpu.roll(p_sum, 112, axis=1)], axis=0)
-    wide = jnp.concatenate([tall, jnp.zeros((112, 128), F32)], axis=0).T
+    tall = []
+    for i in range(2):
+        wide = jnp.broadcast_to(p_sum[i], (8, 128))
+        rows = wide
+        for j in range(1, 8):
+            rows = jnp.where(sub == j, pltpu.roll(wide, 128 - 16 * j, axis=1), rows)
+        tall.append(rows)
+    wide = jnp.concatenate(tall + [jnp.zeros((112, 128), F32)], axis=0).T
     per_ref[0] = wide[0:8, 0:16]
     per_ref[1] = wide[8:16, 0:16]
 
@@ -492,9 +530,9 @@
     sol, cor, per = pl.pallas_call(
         functools.partial(kernel, sizes),
         out_shape=(
-            jax.ShapeDtypeStruct((192, 128), F32),
-            jax.ShapeDtypeStruct((96, 128), F32),
-            jax.ShapeDtypeStruct((2, 8, 16), F32),
+            pltpu.VMEM((192, 128), F32),
+            pltpu.VMEM((96, 128), F32),
+            pltpu.VMEM((2, 8, 16), F32),
         ),
         in_specs=[pl.BlockSpec(memory_space=pltpu.SMEM), anywhere, anywhere, anywhere],
         out_specs=(vmem, vmem, vmem),
@@ -515,15 +553,14 @@
             pltpu.VMEM((n_it, 2, 2, 2, 3, 8, 128), F32),
             pltpu.VMEM((n_it, 2, 2, 3, 8, 128), F32),
             pltpu.VMEM((n_it, 2, 2, 3, 8, 128), F32),
-            pltpu.VMEM((2, 6, 128, 1536), BF16),
+            pltpu.VMEM((2, 2, 128, 1536), BF16),
             pltpu.VMEM((2, 3, 18, 256), F32),
-            pltpu.VMEM((256, 1024), BF16),
             pltpu.VMEM((768, 3072), BF16),
             pltpu.VMEM((128, 3072), BF16),
             pltpu.VMEM((16, 16, 768), BF16),
             pltpu.VMEM((16, 16, 768), BF16),
-            pltpu.VMEM((16, 8, 128), F32),
-            pltpu.VMEM((16, 8, 128), F32),
+            pltpu.VMEM((16, 2, 1, 128), F32),
+            pltpu.VMEM((16, 2, 1, 128), F32),
             dma((n_it, 2)), dma((n_it, 2)), dma((n_it, 2)), dma((n_it, 2)),
             dma((2,)), dma((2,)), dma(()), dma(()), dma((3,)),
             dma((8,)), dma((8,)), dma((8,)), dma((8,)),

time: 47.6 us -> 43.6 us (0.916); the launches traced: 47.4 us -> 42.8 us
  Pallas kernels: 43.9 us -> 40.3 us
  local copies, waits for them, and re-layouts: 2.85 us -> 1.86 us
    pallas_call x1, Pallas kernels: 43.9 us -> 40.3 us  [body(): pl.pallas_call(functools.partial(kernel, sizes), out_shape=(pltpu.VMEM((1...]
    unnamed x7 -> x3, local copies, waits for them, and re-layouts: 2.85 us -> 1.86 us
where the time goes in v2:
time: 43.6 us; the launch traced here: 42.8 us
  Pallas kernels  40.3 us (92%)
  local copies, waits for them, and re-layouts  1.86 us (4%)
  between operations  0.64 us (1%)
    pallas_call x1, Pallas kernels, body(): pl.pallas_call(functools.partial(kernel, sizes), out_shape=(pltpu.VMEM((1...  40.3 us
    unnamed x3, local copies, waits for them, and re-layouts  1.86 us

profile of v2, /device:TPU:81, one launch (start us, length us, event | category | flops | bytes accessed | tf_op | source)
XLA Modules:
  0.0 42.8 jit_solution(12911594088607660204)
XLA Ops:
  0.6 40.3 %shard_map.67 = (f32[192,128]{1,0:T(8,128)S(1)}, f32[96,128]{1,0:T(8,128)S(1)}, f32[2,8,16]{2,1,0:T(8,128)S(1)}) custom-call(f32[4]{0:T(128)} %al_ref.1, f32[192,128]{1,0:T(8,128)} %bitcast.29, f32[288,128]{1,0:T(8,128)} %bitcast.28, bf16[3072,128]{1,0:T(8,128)(2,1)} %bitcast.27), custom_call_target="tpu_custom_call" | custom-call | tf_op jit(solution)/shard_map/pallas_call | solution.py:530
  40.9 0.6 %copy.14 = f32[2,24,1,2,256]{4,3,2,1,0:T(2,128)} copy(f32[2,24,1,2,256]{4,3,2,1,0:T(2,128)S(1)} %bitcast.24) | data formatting | bytes 196608
  41.5 0.6 %copy.15 = f32[1,16,3,2,128]{4,3,2,1,0:T(2,128)} copy(f32[1,16,3,2,128]{4,3,2,1,0:T(2,128)S(1)} %bitcast.25) | data formatting | bytes 98304
  42.2 0.6 %copy.16 = f32[1,16,2,8]{1,3,2,0:T(8,128)} copy(f32[1,16,2,8]{1,3,2,0:T(8,128)S(1)} %bitcast.26) | data formatting | bytes 2048

commit v3 on v2

--- a/solution.py
+++ b/solution.py
@@ -88,14 +88,16 @@
     sol_ref, cor_ref, per_ref,
     rs_v, lk_v, vraw, v32, vall, relay, u8, lz, uz,
     res, total, hsum, tsend, trecv, zsend, zrecv, w_ref, ub_ref, g_ref, s_ref,
-    csend, crecv, psend, precv,
+    cpart, csib, cmsg, cown, crecv, psend, precv, pwork,
     t_ss, t_rs, z_ss, z_rs, vh_ss, vh_rs, uh_ss, uh_rs, loc_s,
-    o_ss, o_rs, r_ss, r_rs, c_ss, c_rs, p_ss, p_rs,
+    o_ss, o_rs, r_ss, r_rs, b_ss, b_rs, c_ss, c_rs, p_ss, p_rs,
 ):
     n_grp, n_ta, n_xyz, scale = sizes
     grp = lax.axis_index("grp")
     ta = lax.axis_index("ta")
     me = lax.axis_index("xyz")
+    chip, core = me // 2, me % 2
+    n_chip = n_xyz // 2
     half_ta = n_ta // 2
     y = grp * 2 + ta // half_ta
     x = ta % half_ta
@@ -134,7 +136,7 @@
         )
 
     def way(c):
-        return y_device(1 - 2 * ((c // 2) % 2))
+        return y_device(1 - 2 * (c % 2))
 
     def own_copy(c):
         rows = pl.ds(pl.multiple_of(c * 384, 384), 384)
@@ -142,7 +144,7 @@
 
     pl.semaphore_wait(barrier, n_xyz - 1 + 4)
     own_copy(0).start()
-    own_copy(2).start()
+    own_copy(1).start()
 
     lane = lax.broadcasted_iota(jnp.int32, (8, 128), 1)
     sub = lax.broadcasted_iota(jnp.int32, (8, 128), 0)
@@ -234,6 +236,8 @@
                 new = old - step * (old - HOPPING * acc[s][p])
                 put(res, s, p, new)
                 put(total, s, p, sums[s][p] + step_after * new)
+
+    vall[256:352, :] = jnp.zeros((96, 3072), BF16)
 
     fetches[0].wait()
     fetches[1].wait()
@@ -266,22 +270,23 @@
         return remote(relay.at[c], vraw.at[1, rows], r_ss.at[c], r_rs.at[c], way(c))
 
     def pass_on(step):
-        for c in (step + 2 * (step // 2), step + 2 * (step // 2) + 2):
+        for c in (2 * step, 2 * step + 1):
             own_copy(c).wait()
             relay_copy(c).start()
 
     def sort_chunk(which, c):
         v32[...] = vraw[which, pl.ds(pl.multiple_of(c * 384, 384), 384), :].astype(F32)
-        rows = pl.ds(pl.multiple_of(c * 16, 16), 16)
+        rows = pl.ds(pl.multiple_of(which * 128 + c * 16, 16), 16)
         for m in range(6):
             for h in range(2):
                 for z in range(2):
                     k = (z * 6 + m) * 256 + h * 128
-                    vall[which, rows, k : k + 128] = v32[
+                    vall[rows, k : k + 128] = v32[
                         pl.ds(4 * m + 2 * h + z, 16, stride=24), :
                     ].astype(BF16)
 
-    low, high = vall.at[0, :, pl.ds(0, 1536)], vall.at[0, :, pl.ds(1536, 1536)]
+    own = pl.ds(0, 128)
+    low, high = vall.at[own, pl.ds(0, 1536)], vall.at[own, pl.ds(1536, 1536)]
     halo_copies = (
         remote(low, w_ref.at[1, 0], vh_ss.at[0], vh_rs.at[0], z_prev),
         remote(high, w_ref.at[0, 1], vh_ss.at[1], vh_rs.at[1], z_next),
@@ -304,12 +309,12 @@
             def _(kc):
                 rows = pl.ds(pl.multiple_of(kc * 16, 16), 16)
 
-                def own(m, side):
-                    return vall[0, rows, part(z * 6 + m, side)]
+                def here(m, side):
+                    return vall[rows, part(z * 6 + m, side)]
 
                 def neighbours(m):
                     if d == 0:
-                        v = own(m, h)
+                        v = here(m, h)
                         column = lane16 % SX
                         return (
                             jnp.where(
@@ -324,7 +329,7 @@
                             ),
                         )
                     if d == 1:
-                        v, w = own(m, h), own(m, 1 - h)
+                        v, w = here(m, h), here(m, 1 - h)
                         up, down = 128 - SX, SX
                         return (
                             jnp.where(
@@ -373,40 +378,22 @@
                     g_ref[below, part(z * 6 + a)] = im
                     g_ref[below, part(z * 6 + 3 + a)] = -re
 
-    def c_copy(target, o):
+    def sibling_copy(k, i):
         return remote(
-            csend.at[target], crecv.at[o], c_ss.at[o], c_rs.at[o], (grp, ta, target)
+            cpart.at[2 * k + 1 - core], csib.at[i], b_ss.at[i], b_rs.at[i],
+            (grp, ta, me + 1 - 2 * core),
+        )
+
+    def c_copy(i):
+        o = (i - chip + n_chip) % n_chip
+        return remote(
+            cmsg.at[i], crecv.at[o], c_ss.at[o], c_rs.at[o], (grp, ta, 2 * i + core)
         )
 
     def p_copy(target, o):
         return remote(
             psend.at[target], precv.at[o], p_ss.at[o], p_rs.at[o], (grp, ta, target)
         )
-
-    def send(copy_of, first, count):
-        @pl.loop(0, count)
-        def _(i):
-            target = first + i
-            o = (target - me + n_xyz) % n_xyz
-
-            @pl.when(o != 0)
-            def _():
-                copy_of(target, o).start()
-
-    def correlate(vectors, first):
-        count = vectors.shape[0] // 16
-        for d in range(3):
-            c = dot_nt(g_ref[256 * d : 256 * (d + 1), :], vectors).T.astype(BF16)
-            csend[pl.ds(first, count), :, 256 * d : 256 * (d + 1)] = c.reshape(count, 16, 256)
-        send(c_copy, first, count)
-
-    def overlap(vectors, first):
-        count = vectors.shape[0] // 16
-        p = dot_nt(vectors, s_ref[...]).reshape(2 * count, 8, 128)
-        p = jnp.where((lane // 16 == sub)[None], p, 0.0)
-        p = jnp.sum(p, axis=1, keepdims=True)
-        psend[pl.ds(first, count)] = p.reshape(count, 2, 1, 128)
-        send(p_copy, first, count)
 
     @pl.loop(0, ITERS - 1)
     def _(n):
@@ -418,7 +405,7 @@
         def _():
             @pl.loop(2, 8)
             def _(i):
-                own_copy(i // 4 * 4 + (i % 2) * 2 + (i // 2) % 2).start()
+                own_copy(i).start()
 
         local_hops()
 
@@ -441,17 +428,15 @@
 
         @pl.when(n == 2)
         def _():
+            pass_on(2)
             for copy in halo_copies:
                 copy.wait()
             gradient(2)
-            correlate(vall[0], grp * 8)
-
-        pass_on(n)
+
+        pass_on(n + n // 2)
         for copy in t_copies(n):
             copy.wait()
         finish(n)
-
-    pass_on(3)
 
     row = lax.broadcasted_iota(jnp.int32, (96, 48), 0)
     col = lax.broadcasted_iota(jnp.int32, (96, 48), 1)
@@ -478,30 +463,72 @@
             rows = placed[16 * m : 16 * m + 16]
             s_ref[:, (z * 6 + m) * 256 : (z * 6 + m + 1) * 256] = jnp.concatenate([rows] * 8)
 
-    overlap(vall[0], grp * 8)
-
-    @pl.loop(0, 2)
-    def _(half):
-        @pl.loop(0, 4)
-        def _(j):
-            relay_copy(4 * half + j).wait()
-            sort_chunk(1, 4 * half + j)
-
-        first = (1 - grp) * 8 + half * 4
-        vectors = vall[1, pl.ds(pl.multiple_of(half * 64, 64), 64), :]
-        correlate(vectors, first)
-        overlap(vectors, first)
+    @pl.loop(0, 3)
+    def _(phase):
+        late = phase // 2
+        start, count = 6 * late, 8 - 2 * phase - 2 * late
+
+        @pl.when(phase > 0)
+        def _():
+            @pl.loop(start, start + count)
+            def _(c):
+                relay_copy(c).wait()
+                sort_chunk(1, c)
+
+        half = jnp.where(phase == 0, grp, 1 - grp)
+        first = half * 8 + start
+        vectors = vall[pl.ds(pl.multiple_of(128 * phase - 32 * late, 32), 128), :]
+        for d in range(3):
+            c = dot_nt(g_ref[256 * d : 256 * (d + 1), :], vectors).T
+            cpart[:, :, 256 * d : 256 * (d + 1)] = c.reshape(8, 16, 256)
+
+        @pl.loop(0, count // 2)
+        def _(k):
+            sibling_copy(k, first // 2 + k).start()
+
+        p = dot_nt(vectors, s_ref[...]).reshape(16, 8, 128)
+        p = jnp.where((lane // 16 == sub)[None], p, 0.0)
+        p = jnp.sum(p, axis=1, keepdims=True)
+        pwork[...] = p.reshape(8, 2, 1, 128)
+
+        @pl.loop(0, count)
+        def _(k):
+            target = first + k
+            o = (target - me + n_xyz) % n_xyz
+            psend[target] = pwork[k]
+
+            @pl.when(o != 0)
+            def _():
+                p_copy(target, o).start()
+
+        @pl.loop(0, count // 2)
+        def _(k):
+            i = first // 2 + k
+            sibling_copy(k, i).wait()
+            both = cpart[2 * k + core] + csib[i]
+
+            @pl.when(i == chip)
+            def _():
+                cown[...] = both
+
+            @pl.when(i != chip)
+            def _():
+                cmsg[i] = both.astype(BF16)
+                c_copy(i).start()
 
     @pl.loop(1, n_xyz)
     def _(o):
-        target = (me + o) % n_xyz
-        c_copy(target, o).wait()
-        p_copy(target, o).wait()
-
-    c_sum = csend[me].astype(F32)
+        p_copy((me + o) % n_xyz, o).wait()
+
+    @pl.loop(1, n_chip)
+    def _(o):
+        c_copy((chip + o) % n_chip).wait()
+
+    c_sum = cown[...]
+    for o in range(1, n_chip):
+        c_sum = c_sum + crecv[o].astype(F32)
     p_sum = psend[me]
     for o in range(1, n_xyz):
-        c_sum = c_sum + crecv[o].astype(F32)
         p_sum = p_sum + precv[o]
     for k in range(6):
         cor_ref[pl.ds(k, 16, stride=6), :] = c_sum[:, 128 * k : 128 * (k + 1)] * scale
@@ -541,7 +568,7 @@
             pltpu.VMEM((288, 128), F32),
             pltpu.VMEM((2, 3072, 128), BF16),
             pltpu.VMEM((384, 128), F32),
-            pltpu.VMEM((2, 128, 3072), BF16),
+            pltpu.VMEM((352, 3072), BF16),
             pltpu.VMEM((8, 384, 128), BF16),
             pltpu.VMEM((576, 128), F32),
             pltpu.VMEM((2, 3, 18, 256), F32),
@@ -557,14 +584,18 @@
             pltpu.VMEM((2, 3, 18, 256), F32),
             pltpu.VMEM((768, 3072), BF16),
             pltpu.VMEM((128, 3072), BF16),
-            pltpu.VMEM((16, 16, 768), BF16),
-            pltpu.VMEM((16, 16, 768), BF16),
+            pltpu.VMEM((8, 16, 768), F32),
+            pltpu.VMEM((8, 16, 768), F32),
+            pltpu.VMEM((8, 16, 768), BF16),
+            pltpu.VMEM((16, 768), F32),
+            pltpu.VMEM((8, 16, 768), BF16),
             pltpu.VMEM((16, 2, 1, 128), F32),
             pltpu.VMEM((16, 2, 1, 128), F32),
+            pltpu.VMEM((8, 2, 1, 128), F32),
             dma((n_it, 2)), dma((n_it, 2)), dma((n_it, 2)), dma((n_it, 2)),
             dma((2,)), dma((2,)), dma(()), dma(()), dma((3,)),
             dma((8,)), dma((8,)), dma((8,)), dma((8,)),
-            dma((16,)), dma((16,)), dma((16,)), dma((16,)),
+            dma((8,)), dma((8,)), dma((8,)), dma((8,)), dma((16,)), dma((16,)),
         ],
         compiler_params=pltpu.CompilerParams(
             collective_id=0, has_side_effects=True, vmem_limit_bytes=56 * 1024 * 1024

time: 43.6 us -> 42 us (0.963)
  Pallas kernels: 40.3 us -> 38.8 us
    pallas_call x1, Pallas kernels: 40.3 us -> 38.8 us  [body(): pl.pallas_call(functools.partial(kernel, sizes), out_shape=(pltpu.VMEM((1...]
where the time goes in v3:
time: 42 us; the launch traced here: 41.3 us
  Pallas kernels  38.8 us (92%)
  local copies, waits for them, and re-layouts  1.86 us (4%)
  between operations  0.64 us (2%)
    pallas_call x1, Pallas kernels, body(): pl.pallas_call(functools.partial(kernel, sizes), out_shape=(pltpu.VMEM((1...  38.8 us
    unnamed x3, local copies, waits for them, and re-layouts  1.86 us

profile of v3, /device:TPU:81, one launch (start us, length us, event | category | flops | bytes accessed | tf_op | source)
XLA Modules:
  0.0 41.3 jit_solution(12963180955587767894)
XLA Ops:
  0.6 38.8 %shard_map.67 = (f32[192,128]{1,0:T(8,128)S(1)}, f32[96,128]{1,0:T(8,128)S(1)}, f32[2,8,16]{2,1,0:T(8,128)S(1)}) custom-call(f32[4]{0:T(128)} %al_ref.1, f32[192,128]{1,0:T(8,128)} %bitcast.29, f32[288,128]{1,0:T(8,128)} %bitcast.28, bf16[3072,128]{1,0:T(8,128)(2,1)} %bitcast.27), custom_call_target="tpu_custom_call" | custom-call | tf_op jit(solution)/shard_map/pallas_call | solution.py:557
  39.5 0.6 %copy.14 = f32[2,24,1,2,256]{4,3,2,1,0:T(2,128)} copy(f32[2,24,1,2,256]{4,3,2,1,0:T(2,128)S(1)} %bitcast.24) | data formatting | bytes 196608
  40.1 0.6 %copy.15 = f32[1,16,3,2,128]{4,3,2,1,0:T(2,128)} copy(f32[1,16,3,2,128]{4,3,2,1,0:T(2,128)S(1)} %bitcast.25) | data formatting | bytes 98304
  40.7 0.6 %copy.16 = f32[1,16,2,8]{1,3,2,0:T(8,128)} copy(f32[1,16,2,8]{1,3,2,0:T(8,128)S(1)} %bitcast.26) | data formatting | bytes 2048

commit v4 on v3

--- a/solution.py
+++ b/solution.py
@@ -182,16 +182,21 @@
 
     def prepare(n):
         psi = spins(res)
-        re, im = project(psi, 3, -1)
-        tsend[n, 0, 0], tsend[n, 0, 1] = re, im
-        re, im = colour(links_of(3), *project(psi, 3, 1), True)
-        tsend[n, 1, 0], tsend[n, 1, 1] = re, im
+
+        def rows(re, im):
+            both = jnp.stack([re, im])
+            return both.reshape(both.size // 128, 128).astype(BF16)
+
+        tsend[n, 0] = rows(*project(psi, 3, -1))
+        tsend[n, 1] = rows(*colour(links_of(3), *project(psi, 3, 1), True))
         re, im = project(psi, 2, -1)
-        zsend[n, 0, 0] = jnp.where(z_is0, re[0], roll(re[1], 1, 0))
-        zsend[n, 0, 1] = jnp.where(z_is0, im[0], roll(im[1], 1, 0))
+        zsend[n, 0] = rows(
+            jnp.where(z_is0, re[0], roll(re[1], 1, 0)), jnp.where(z_is0, im[0], roll(im[1], 1, 0))
+        )
         re, im = colour(links_of(2), *project(psi, 2, 1), True)
-        zsend[n, 1, 0] = jnp.where(z_is0, roll(re[1], 7, 0), re[0])
-        zsend[n, 1, 1] = jnp.where(z_is0, roll(im[1], 7, 0), im[0])
+        zsend[n, 1] = rows(
+            jnp.where(z_is0, roll(re[1], 7, 0), re[0]), jnp.where(z_is0, roll(im[1], 7, 0), im[0])
+        )
 
     def local_hops():
         psi = spins(res)
@@ -211,23 +216,25 @@
         sums = spins(total)
         sign_up = jnp.where(ta == n_ta - 1, -1.0, 1.0).astype(F32)
         sign_down = jnp.where(ta == 0, -1.0, 1.0).astype(F32)
+        from_z = [zrecv[n, k].astype(F32).reshape(2, 3, 8, 128) for k in range(2)]
+        from_t = [trecv[n, k].astype(F32).reshape(2, 2, 3, 8, 128) for k in range(2)]
         re, im = project(psi, 2, -1)
 
         def ahead(v, got):
             return jnp.where(z_is0, roll(v, 7, 0), jnp.stack([roll(got, 1, 0), got]))
 
-        re, im = ahead(re, zrecv[n, 0, 0]), ahead(im, zrecv[n, 0, 1])
+        re, im = ahead(re, from_z[0][0]), ahead(im, from_z[0][1])
         rebuild(acc, *colour(links_of(2), re, im, False), 2, -1)
         re, im = colour(links_of(2), *project(psi, 2, 1), True)
 
         def behind(v, got):
             return jnp.where(z_is0, jnp.stack([roll(got, 7, 0), got]), roll(v, 1, 0))
 
-        re, im = behind(re, zrecv[n, 1, 0]), behind(im, zrecv[n, 1, 1])
+        re, im = behind(re, from_z[1][0]), behind(im, from_z[1][1])
         rebuild(acc, re, im, 2, 1)
-        re, im = trecv[n, 0, 0] * sign_up, trecv[n, 0, 1] * sign_up
+        re, im = from_t[0][0] * sign_up, from_t[0][1] * sign_up
         rebuild(acc, *colour(links_of(3), re, im, False), 3, -1)
-        rebuild(acc, trecv[n, 1, 0] * sign_down, trecv[n, 1, 1] * sign_down, 3, 1)
+        rebuild(acc, from_t[1][0] * sign_down, from_t[1][1] * sign_down, 3, 1)
         step = al_ref[n]
         step_after = al_ref[n + 1]
         for s in range(4):
@@ -395,12 +402,57 @@
             psend.at[target], precv.at[o], p_ss.at[o], p_rs.at[o], (grp, ta, target)
         )
 
+    def correlate(vectors, first, count):
+        for d in range(3):
+            c = dot_nt(g_ref[256 * d : 256 * (d + 1), :], vectors).T
+            cpart[:, :, 256 * d : 256 * (d + 1)] = c.reshape(8, 16, 256)
+
+        @pl.loop(0, count // 2)
+        def _(k):
+            sibling_copy(k, first // 2 + k).start()
+
+    def combine(first, count):
+        @pl.loop(0, count // 2)
+        def _(k):
+            i = first // 2 + k
+            sibling_copy(k, i).wait()
+            both = cpart[2 * k + core] + csib[i]
+
+            @pl.when(i == chip)
+            def _():
+                cown[...] = both
+
+            @pl.when(i != chip)
+            def _():
+                cmsg[i] = both.astype(BF16)
+                c_copy(i).start()
+
+    def overlap(vectors, first, count):
+        p = dot_nt(vectors, s_ref[...]).reshape(16, 8, 128)
+        p = jnp.where((lane // 16 == sub)[None], p, 0.0)
+        p = jnp.sum(p, axis=1, keepdims=True)
+        pwork[...] = p.reshape(8, 2, 1, 128)
+
+        @pl.loop(0, count)
+        def _(k):
+            target = first + k
+            o = (target - me + n_xyz) % n_xyz
+            psend[target] = pwork[k]
+
+            @pl.when(o != 0)
+            def _():
+                p_copy(target, o).start()
+
     @pl.loop(0, ITERS - 1)
     def _(n):
         prepare(n)
         for copy in t_copies(n):
             copy.start()
 
+        @pl.when(n > 0)
+        def _():
+            pass_on(n - 1)
+
         @pl.when(n == 0)
         def _():
             @pl.loop(2, 8)
@@ -428,12 +480,14 @@
 
         @pl.when(n == 2)
         def _():
-            pass_on(2)
             for copy in halo_copies:
                 copy.wait()
             gradient(2)
-
-        pass_on(n + n // 2)
+            pass_on(2)
+            correlate(vall[0:128, :], grp * 8, 8)
+            pass_on(3)
+            combine(grp * 8, 8)
+
         for copy in t_copies(n):
             copy.wait()
         finish(n)
@@ -463,58 +517,22 @@
             rows = placed[16 * m : 16 * m + 16]
             s_ref[:, (z * 6 + m) * 256 : (z * 6 + m + 1) * 256] = jnp.concatenate([rows] * 8)
 
-    @pl.loop(0, 3)
-    def _(phase):
-        late = phase // 2
-        start, count = 6 * late, 8 - 2 * phase - 2 * late
-
-        @pl.when(phase > 0)
-        def _():
-            @pl.loop(start, start + count)
-            def _(c):
-                relay_copy(c).wait()
-                sort_chunk(1, c)
-
-        half = jnp.where(phase == 0, grp, 1 - grp)
-        first = half * 8 + start
-        vectors = vall[pl.ds(pl.multiple_of(128 * phase - 32 * late, 32), 128), :]
-        for d in range(3):
-            c = dot_nt(g_ref[256 * d : 256 * (d + 1), :], vectors).T
-            cpart[:, :, 256 * d : 256 * (d + 1)] = c.reshape(8, 16, 256)
-
-        @pl.loop(0, count // 2)
-        def _(k):
-            sibling_copy(k, first // 2 + k).start()
-
-        p = dot_nt(vectors, s_ref[...]).reshape(16, 8, 128)
-        p = jnp.where((lane // 16 == sub)[None], p, 0.0)
-        p = jnp.sum(p, axis=1, keepdims=True)
-        pwork[...] = p.reshape(8, 2, 1, 128)
-
-        @pl.loop(0, count)
-        def _(k):
-            target = first + k
-            o = (target - me + n_xyz) % n_xyz
-            psend[target] = pwork[k]
-
-            @pl.when(o != 0)
-            def _():
-                p_copy(target, o).start()
-
-        @pl.loop(0, count // 2)
-        def _(k):
-            i = first // 2 + k
-            sibling_copy(k, i).wait()
-            both = cpart[2 * k + core] + csib[i]
-
-            @pl.when(i == chip)
-            def _():
-                cown[...] = both
-
-            @pl.when(i != chip)
-            def _():
-                cmsg[i] = both.astype(BF16)
-                c_copy(i).start()
+    overlap(vall[0:128, :], grp * 8, 8)
+
+    @pl.loop(0, 2)
+    def _(late):
+        start, count = 6 * late, 6 - 4 * late
+
+        @pl.loop(start, start + count)
+        def _(c):
+            relay_copy(c).wait()
+            sort_chunk(1, c)
+
+        first = (1 - grp) * 8 + start
+        vectors = vall[pl.ds(pl.multiple_of(128 + 96 * late, 32), 128), :]
+        correlate(vectors, first, count)
+        overlap(vectors, first, count)
+        combine(first, count)
 
     @pl.loop(1, n_xyz)
     def _(o):
@@ -576,10 +594,10 @@
             pltpu.VMEM((192, 128), F32),
             pltpu.VMEM((192, 128), F32),
             pltpu.VMEM((192, 128), F32),
-            pltpu.VMEM((n_it, 2, 2, 2, 3, 8, 128), F32),
-            pltpu.VMEM((n_it, 2, 2, 2, 3, 8, 128), F32),
-            pltpu.VMEM((n_it, 2, 2, 3, 8, 128), F32),
-            pltpu.VMEM((n_it, 2, 2, 3, 8, 128), F32),
+            pltpu.VMEM((n_it, 2, 96, 128), BF16),
+            pltpu.VMEM((n_it, 2, 96, 128), BF16),
+            pltpu.VMEM((n_it, 2, 48, 128), BF16),
+            pltpu.VMEM((n_it, 2, 48, 128), BF16),
             pltpu.VMEM((2, 2, 128, 1536), BF16),
             pltpu.VMEM((2, 3, 18, 256), F32),
             pltpu.VMEM((768, 3072), BF16),

time: 42 us -> 40.4 us (0.962)
  Pallas kernels: 38.8 us -> 37.3 us
    pallas_call x1, Pallas kernels: 38.8 us -> 37.3 us  [body(): pl.pallas_call(functools.partial(kernel, sizes), out_shape=(pltpu.VMEM((1...]
where the time goes in v4:
time: 40.4 us; the launch traced here: 39.8 us
  Pallas kernels  37.3 us (92%)
  local copies, waits for them, and re-layouts  1.86 us (5%)
  between operations  0.64 us (2%)
    pallas_call x1, Pallas kernels, body(): pl.pallas_call(functools.partial(kernel, sizes), out_shape=(pltpu.VMEM((1...  37.3 us
    unnamed x3, local copies, waits for them, and re-layouts  1.86 us

profile of v4, /device:TPU:81, one launch (start us, length us, event | category | flops | bytes accessed | tf_op | source)
XLA Modules:
  0.0 39.8 jit_solution(406389350442885897)
XLA Ops:
  0.6 37.3 %shard_map.67 = (f32[192,128]{1,0:T(8,128)S(1)}, f32[96,128]{1,0:T(8,128)S(1)}, f32[2,8,16]{2,1,0:T(8,128)S(1)}) custom-call(f32[4]{0:T(128)} %al_ref.1, f32[192,128]{1,0:T(8,128)} %bitcast.29, f32[288,128]{1,0:T(8,128)} %bitcast.28, bf16[3072,128]{1,0:T(8,128)(2,1)} %bitcast.27), custom_call_target="tpu_custom_call" | custom-call | tf_op jit(solution)/shard_map/pallas_call | solution.py:575
  37.9 0.6 %copy.14 = f32[2,24,1,2,256]{4,3,2,1,0:T(2,128)} copy(f32[2,24,1,2,256]{4,3,2,1,0:T(2,128)S(1)} %bitcast.24) | data formatting | bytes 196608
  38.5 0.6 %copy.15 = f32[1,16,3,2,128]{4,3,2,1,0:T(2,128)} copy(f32[1,16,3,2,128]{4,3,2,1,0:T(2,128)S(1)} %bitcast.25) | data formatting | bytes 98304
  39.2 0.6 %copy.16 = f32[1,16,2,8]{1,3,2,0:T(8,128)} copy(f32[1,16,2,8]{1,3,2,0:T(8,128)S(1)} %bitcast.26) | data formatting | bytes 2048

commit v5 on v4

--- a/solution.py
+++ b/solution.py
@@ -486,7 +486,6 @@
             pass_on(2)
             correlate(vall[0:128, :], grp * 8, 8)
             pass_on(3)
-            combine(grp * 8, 8)
 
         for copy in t_copies(n):
             copy.wait()
@@ -518,6 +517,7 @@
             s_ref[:, (z * 6 + m) * 256 : (z * 6 + m + 1) * 256] = jnp.concatenate([rows] * 8)
 
     overlap(vall[0:128, :], grp * 8, 8)
+    combine(grp * 8, 8)
 
     @pl.loop(0, 2)
     def _(late):

time: 40.4 us -> 40.4 us (level)
  no operation moved by 1% of the time
where the time goes in v5:
time: 40.4 us; the launch traced here: 39.8 us
  Pallas kernels  37.3 us (92%)
  local copies, waits for them, and re-layouts  1.86 us (5%)
  between operations  0.64 us (2%)
    pallas_call x1, Pallas kernels, body(): pl.pallas_call(functools.partial(kernel, sizes), out_shape=(pltpu.VMEM((1...  37.3 us
    unnamed x3, local copies, waits for them, and re-layouts  1.86 us

profile of v5, /device:TPU:81, one launch (start us, length us, event | category | flops | bytes accessed | tf_op | source)
XLA Modules:
  0.0 39.8 jit_solution(1912508844387867796)
XLA Ops:
  0.6 37.3 %shard_map.67 = (f32[192,128]{1,0:T(8,128)S(1)}, f32[96,128]{1,0:T(8,128)S(1)}, f32[2,8,16]{2,1,0:T(8,128)S(1)}) custom-call(f32[4]{0:T(128)} %al_ref.1, f32[192,128]{1,0:T(8,128)} %bitcast.29, f32[288,128]{1,0:T(8,128)} %bitcast.28, bf16[3072,128]{1,0:T(8,128)(2,1)} %bitcast.27), custom_call_target="tpu_custom_call" | custom-call | tf_op jit(solution)/shard_map/pallas_call | solution.py:575
  37.9 0.6 %copy.14 = f32[2,24,1,2,256]{4,3,2,1,0:T(2,128)} copy(f32[2,24,1,2,256]{4,3,2,1,0:T(2,128)S(1)} %bitcast.24) | data formatting | bytes 196608
  38.5 0.6 %copy.15 = f32[1,16,3,2,128]{4,3,2,1,0:T(2,128)} copy(f32[1,16,3,2,128]{4,3,2,1,0:T(2,128)S(1)} %bitcast.25) | data formatting | bytes 98304
  39.2 0.6 %copy.16 = f32[1,16,2,8]{1,3,2,0:T(8,128)} copy(f32[1,16,2,8]{1,3,2,0:T(8,128)S(1)} %bitcast.26) | data formatting | bytes 2048
